TPU v7x, 256 devices: a whole 4x4x8 slice. The times are simulated.
256 devices in a mesh: tp: 8 (over z_hi, core), ex: 8 (over y, z_lo), co: 4 (over x).
Axes of the slice: x: 4, y: 4, z: 8 (z_hi: 4, z_lo: 2; z = z_hi * 2 + z_lo), core: 2. Of those that a mesh axis runs over, the one named last changes fastest.
Arguments:
- query_states: bfloat16 [8192, 4096], P('ex'), may hold values from -6 to 6
- out_cotangent: bfloat16 [8192, 4096], P('ex', ('tp', 'co')), may hold values from -6 to 6
- query_of_token: int32 [8192], P('ex'), may hold values from 0 to 31, as said below
- gate_weight: bfloat16 [4096, 14336], P(None, ('tp', 'co')), may hold values from -0.09375 to 0.09375
- up_weight: bfloat16 [4096, 14336], P(None, ('tp', 'co')), may hold values from -0.09375 to 0.09375
- proj_in: bfloat16 [14336, 128], P(('tp', 'co')), may hold values from -0.19209402 to 0.19209402, as said below
- proj_out: bfloat16 [4096, 128], P(('tp', 'co')), may hold values from -0.09375 to 0.09375
- database: bfloat16 [8192, 16384], P('ex', ('tp', 'co')), may hold values from -6 to 6
- stored_ids: int32 [8192], P('ex'), may hold values from 0 to 8191, each once
Outputs:
- solution: float32 [16384, 32], P(('tp', 'co'))
- scores: float32 [8192, 32], P('ex')
Inputs may be any that keep to these rules, and one draw needn't show every extreme that they name: `query_of_token`: the tokens in rows b * 1024 to (b + 1) * 1024 - 1 belong to queries b * 4 to (b + 1) * 4 - 1, and every query has at least one token. `stored_ids`: every example id appears exactly once. `proj_in`: every entry lies within plus or minus 23 * 14336 ** -0.5.
All inputs are finite; a program needn't handle non-finite values.
Results may differ from a plain program's by a relative error of at most 0.03.
Values sent between devices are 32-bit elements; how exact they have to be, the bound alone decides.
A program may use at most 64 MiB of HBM per device.

v0:
```python
import math

import jax
import jax.numpy as jnp
from jax import lax
from jax.sharding import Mesh
from jax.sharding import PartitionSpec as P

ROUT = 128
K = 16384
QPG = 4
ITERS = 2
TP_CO = ("tp_0", "tp_1", "co")


DAMPING = 1.0
HIGHEST = lax.Precision.HIGHEST


def from_everyone(value, axis):
    devices = lax.axis_size(axis)
    return lax.all_to_all(
        jnp.broadcast_to(value[None], (devices, *value.shape)), axis, 0, 0, tiled=True
    )


def of_everyone(value, axis):
    return from_everyone(value, axis).sum(axis=0)


def split_up(value, dim, devices):
    before, after = (value.shape[:dim], value.shape[dim + 1 :])
    return jnp.moveaxis(value.reshape(*before, devices, -1, *after), dim, 0)


def sent_and_summed(value, axis, dim):
    devices = lax.axis_size(axis)
    pieces = lax.all_to_all(split_up(value, dim, devices), axis, 0, 0, tiled=True)
    return jnp.sum(pieces, axis=0)


def sum_by_axis(value, axes, dim):
    far, near = axes
    pieces = split_up(value, dim, lax.axis_size(far))
    nearer = sent_and_summed(pieces, near, dim + 1)
    arrived = lax.all_to_all(nearer, far, split_axis=0, concat_axis=0, tiled=True)
    return arrived.sum(axis=0)


def filled_up(lines, devices):
    spare = -lines.shape[0] % devices
    if not spare:
        return lines
    return jnp.concatenate([lines, jnp.zeros((spare, *lines.shape[1:]), lines.dtype)])


def joined_along(pieces, dim):
    pieces = jnp.moveaxis(pieces, 0, dim)
    dims = pieces.shape
    return pieces.reshape(*dims[:dim], dims[dim] * dims[dim + 1], *dims[dim + 2 :])


def gathered_by_axis(value, axes, dim):
    far, near = axes
    pieces = from_everyone(from_everyone(value, far), near)
    return joined_along(pieces.swapaxes(0, 1).reshape(-1, *value.shape), dim)


def sum_by_parts(value, axes):
    own = sum_by_axis(filled_up(value, lax.axis_size(axes[0]) * lax.axis_size(axes[1])), axes, 0)
    whole = gathered_by_axis(own, axes, 0)
    return whole[: len(value)].reshape(value.shape)


def in_one(arrays, axis):
    ravelled, at, outs = (jnp.concatenate([a.reshape(-1) for a in arrays]), 0, [])
    so_far = sum_by_parts(ravelled, axis)
    for a in arrays:
        outs.append(so_far[at : at + a.size].reshape(a.shape))
        at += a.size
    return tuple(outs)


def gather_directly(value, axis, dim):
    pieces = from_everyone(value, axis)
    return joined_along(pieces, dim)


def nested_sum(value, axes):
    own = sent_and_summed(filled_up(value, lax.axis_size(axes)), axes, 0)
    whole = gather_directly(own, axes, 0)
    return whole[: len(value)].reshape(value.shape)


def in_one_2(arrays, axis):
    ends = [0]
    for a in arrays:
        ends.append(ends[-1] + a.size)
    so_far = nested_sum(jnp.concatenate([a.ravel() for a in arrays]), axis)
    return tuple((so_far[b:e].reshape(a.shape) for a, b, e in zip(arrays, ends, ends[1:])))


def together(arrays, axis):
    ends = [0]
    for a in arrays:
        ends.append(ends[-1] + a.size)
    so_far = of_everyone(jnp.concatenate([a.ravel() for a in arrays]), axis)
    return tuple((so_far[b:e].reshape(a.shape) for a, b, e in zip(arrays, ends, ends[1:])))


def total_of(value, axes):
    lines = value.reshape(-1, value.shape[-1])
    own = sent_and_summed(filled_up(lines, lax.axis_size(axes)), axes, 0)
    whole = gather_directly(own, axes, 0)
    return whole[: len(lines)].reshape(value.shape)


def in_one_piece(arrays, axis, dim, along):
    columns = [a.reshape(*a.shape[:along], -1) for a in arrays]
    both = jnp.concatenate(columns, axis=along)
    whole, at, outs = (lax.all_gather(both, axis, axis=dim, tiled=True), 0, [])
    for a, column in zip(arrays, columns):
        piece = whole[..., at : at + column.shape[along]]
        outs.append(piece.reshape(*piece.shape[:along], *a.shape[along:]))
        at += column.shape[along]
    return tuple(outs)


def inner_gram(first, second):
    return lax.dot_general(
        first,
        second,
        (((0,), (0,)), ((), ())),
        precision=HIGHEST,
        preferred_element_type=jnp.float32,
    )


def times_small(matrix, coeffs):
    return jnp.dot(matrix, coeffs, precision=HIGHEST, preferred_element_type=jnp.float32)


def solve_spd(matrix, target):
    factor = jnp.linalg.cholesky(matrix)
    return jax.scipy.linalg.cho_solve((factor, True), target)


def symmetric(matrix):
    return 0.5 * (matrix + matrix.T)


def residual_gram(residual):
    return of_everyone(inner_gram(residual, residual), TP_CO)


def outer_grads(left_cols, right_full, onehot):
    tokens = left_cols.shape[0]
    columns = left_cols.shape[1]
    per_query = onehot.shape[1]
    weighted = (left_cols[:, :, None] * onehot[:, None, :]).reshape(tokens, columns * per_query)
    grads = inner_gram(weighted, right_full)
    return (
        grads.reshape(columns, per_query, ROUT)
        .transpose(0, 2, 1)
        .reshape(columns * ROUT, per_query)
    )


def local(
    query_states,
    out_cotangent,
    query_of_token,
    gate_weight,
    up_weight,
    proj_in,
    proj_out,
    database,
    stored_ids,
):
    learners = lax.axis_size(TP_CO)
    learner = lax.axis_index(TP_CO)
    ex_count = lax.axis_size("ex")
    ex_index = lax.axis_index("ex")
    band_cols = proj_in.shape[1] // learners
    local_ids = query_of_token - ex_index * QPG
    onehot = (local_ids[:, None] == jnp.arange(QPG, dtype=jnp.int32)[None, :]).astype(jnp.float32)
    right_part = jnp.dot(out_cotangent, proj_out, preferred_element_type=jnp.float32)
    gate_act = jnp.dot(query_states, gate_weight, preferred_element_type=jnp.float32)
    up_act = jnp.dot(query_states, up_weight, preferred_element_type=jnp.float32)
    hidden = (jax.nn.silu(gate_act) * up_act).astype(jnp.bfloat16)
    left_part = jnp.dot(hidden, proj_in, preferred_element_type=jnp.float32)
    left_full, right_full = in_one((left_part, right_part), ("tp_0", ("tp_1", "co")))
    left_band = lax.dynamic_slice_in_dim(left_full, learner * band_cols, band_cols, 1)
    local_grads = outer_grads(left_band, right_full, onehot)
    targets = gather_directly(local_grads, "ex", 1)
    rows_local = database.shape[0]
    gram_scale = 1.0 / math.sqrt(float(rows_local * ex_count))
    solution = jnp.zeros_like(targets)
    residual = targets
    direction = targets
    norm_now = residual_gram(residual)
    for step_index in range(ITERS):
        packed = direction.astype(jnp.bfloat16)
        partial_rows = jnp.dot(database, packed, preferred_element_type=jnp.float32)
        row_sums, direction_gram = in_one_2((partial_rows, inner_gram(direction, direction)), TP_CO)
        scaled_rows = row_sums * gram_scale
        rows_low = scaled_rows.astype(jnp.bfloat16)
        back_term = lax.dot_general(
            database, rows_low, (((0,), (0,)), ((), ())), preferred_element_type=jnp.float32
        )
        back_sum, rows_gram = together(
            (back_term, inner_gram(scaled_rows, rows_low.astype(jnp.float32))), "ex"
        )
        image = back_sum * gram_scale + DAMPING * direction
        curvature = symmetric(rows_gram + DAMPING * direction_gram)
        step_size = solve_spd(curvature, norm_now)
        solution = solution + times_small(direction, step_size)
        residual = residual - times_small(image, step_size)
        if step_index + 1 < ITERS:
            norm_next = residual_gram(residual)
            mixing = solve_spd(norm_now, norm_next)
            direction = residual + times_small(direction, mixing)
            norm_now = norm_next
    final_low = solution.astype(jnp.bfloat16)
    score_part = jnp.dot(database, final_low, preferred_element_type=jnp.float32)
    score_rows = total_of(score_part, TP_CO) * (1.0 / math.sqrt(K))
    all_scores, all_ids = in_one_piece((score_rows, stored_ids.astype(jnp.float32)), "ex", 0, 1)
    position = all_ids.astype(jnp.int32) - ex_index * rows_local
    inside = (position >= 0) & (position < rows_local)
    position = jnp.where(inside, position, rows_local)
    placed = (
        jnp.zeros((rows_local, all_scores.shape[1]), jnp.float32)
        .at[position]
        .set(all_scores, mode="drop")
    )
    return (solution, placed)


def solution(mesh):
    finer = Mesh(
        mesh.devices.reshape(4, 2, mesh.shape["ex"], mesh.shape["co"]), ("tp_0", "tp_1", "ex", "co")
    )
    in_specs = (
        P("ex", None),
        P("ex", TP_CO),
        P("ex"),
        P(None, TP_CO),
        P(None, TP_CO),
        P(TP_CO, None),
        P(TP_CO, None),
        P("ex", TP_CO),
        P("ex"),
    )
    out_specs = (P(TP_CO, None), P("ex", None))
    return jax.shard_map(local, mesh=finer, in_specs=in_specs, out_specs=out_specs, check_vma=False)
```

profile of v0, /device:TPU:1, one launch (start us, length us, event | category | flops | bytes accessed | tf_op | source)
XLA Modules:
  0.0 356.4 jit_solution(9248042751843610744)
XLA Ops:
  7.2 1.2 fusion.47
  8.5 0.4 copy.98
  9.0 9.7 %fusion.46 = f32[1024,448]{0,1:T(8,128)} fusion(bf16[1024,4096]{1,0:T(8,128)(2,1)} %param.12, bf16[4096,448]{0,1:T(8,128)(2,1)} %param.15), kind=kOutput, calls=%fused_computation.92 | convolution fusion | flops 3758096384 | bytes 13893632 | tf_op jit(solution)/shard_map/dot_general | solution.py:188
  18.7 9.4 %fusion = f32[1024,128]{1,0:T(8,128)S(1)} fusion(bf16[448,128]{1,0:T(8,128)(2,1)S(1)} %copy-done.4, f32[1024,448]{0,1:T(8,128)} %fusion.46, bf16[1024,4096]{1,0:T(8,128)(2,1)} %param.12, bf16[4096,448]{0,1:T(8,128)(2,1)} %param.16), kind=kOutput, calls=%fused_computation.2 | convolution fusion | flops 3878289408 | bytes 14532608 | tf_op jit(solution)/shard_map/dot_general | solution.py:191
  28.2 0.4 copy.97
  28.6 0.5 maximum_bitcast_fusion
  29.1 20.6 %all_to_all.92 = f32[8,4,8192]{2,1,0:T(4,128)S(1)} all-to-all(f32[8,4,8192]{2,1,0:T(4,128)S(1)} %maximum_bitcast_fusion), channel_id=1, replica_groups=mesh['tp_0'=4,'tp_1'=2,'ex'=8,'co'=4] {'tp_1','co'}, dimensions={0} | all-to-all | bytes 2097152 | tf_op jit(solution)/shard_map/all_to_all | solution.py:38
  50.0 15.2 %all_to_all.93 = f32[4,1,8192]{2,1,0:T(1,128)S(1)} all-to-all(f32[4,1,8192]{2,1,0:T(1,128)S(1)} %all_to_all.60), channel_id=1, replica_groups=mesh['tp_0'=4,'tp_1'=2,'ex'=8,'co'=4] {'tp_0'}, dimensions={0} | all-to-all | bytes 262144 | tf_op jit(solution)/shard_map/all_to_all | solution.py:46
  65.4 9.9 %all_to_all.94 = f32[4,1,8192]{2,1,0:T(1,128)S(1)} all-to-all(f32[4,1,8192]{2,1,0:T(1,128)S(1)} %broadcast_in_dim.27), channel_id=1, replica_groups=mesh['tp_0'=4,'tp_1'=2,'ex'=8,'co'=4] {'tp_0'}, dimensions={0} | all-to-all | bytes 262144 | tf_op jit(solution)/shard_map/all_to_all | solution.py:22
  75.4 1.1 broadcast_in_dim.30
  76.5 7.0 %all-to-all-start.3 = ((f32[8,4,8192]{2,1,0:T(4,128)}), f32[8,4,8192]{2,1,0:T(4,128)S(1)}, u32[]{:S(2)}, u32[]{:S(2)}) async-start(f32[8,4,8192]{2,1,0:T(4,128)} %broadcast_in_dim.30), calls=%async_computation.3 | async-start | bytes 2097152 | tf_op jit(solution)/shard_map/all_to_all | solution.py:22
  83.6 15.0 %all-to-all-done.3 = f32[8,4,8192]{2,1,0:T(4,128)S(1)} async-done(((f32[8,4,8192]{2,1,0:T(4,128)}), f32[8,4,8192]{2,1,0:T(4,128)S(1)}, u32[]{:S(2)}, u32[]{:S(2)}) %all-to-all-start.3) | async-done | bytes 1048608 | tf_op jit(solution)/shard_map/all_to_all | solution.py:22
  98.5 0.4 fusion.45
  100.2 0.4 convolution_bitcast_fusion.5
  100.7 9.6 %all_to_all.95 = f32[8,512,4]{1,2,0:T(4,128)S(1)} all-to-all(f32[8,512,4]{1,2,0:T(4,128)S(1)} %broadcast_in_dim.32), channel_id=1, replica_groups=mesh['tp_0'=4,'tp_1'=2,'ex'=8,'co'=4] {'ex'}, dimensions={0} | all-to-all | bytes 131072 | tf_op jit(solution)/shard_map/all_to_all | solution.py:22
  111.6 16.1 %all_to_all.96 = f32[32,1,1056]{2,1,0:T(1,128)S(1)} all-to-all(f32[32,1,1056]{2,1,0:T(1,128)S(1)} %all_to_all.65), channel_id=1, replica_groups=mesh['tp_0'=4,'tp_1'=2,'ex'=8,'co'=4] {'tp_0','tp_1','co'}, dimensions={0} | all-to-all | bytes 270336 | tf_op jit(solution)/shard_map/all_to_all | solution.py:38
  127.8 0.7 broadcast_in_dim.33
  128.6 4.3 %all-to-all-start.6 = ((f32[32,1,1056]{2,1,0:T(1,128)}), f32[32,1,1056]{2,1,0:T(1,128)S(1)}, u32[]{:S(2)}, u32[]{:S(2)}) async-start(f32[32,1,1056]{2,1,0:T(1,128)} %broadcast_in_dim.33), calls=%async_computation.6 | async-start | bytes 294912 | tf_op jit(solution)/shard_map/all_to_all | solution.py:22
  133.0 0.9 reshape.216
  133.9 10.0 %all-to-all-done.6 = f32[32,1,1056]{2,1,0:T(1,128)S(1)} async-done(((f32[32,1,1056]{2,1,0:T(1,128)}), f32[32,1,1056]{2,1,0:T(1,128)S(1)}, u32[]{:S(2)}, u32[]{:S(2)}) %all-to-all-start.6) | async-done | bytes 135200 | tf_op jit(solution)/shard_map/all_to_all | solution.py:22
  143.9 4.3 %all-to-all-start.8 = ((f32[32,1,1024]{2,1,0:T(1,128)}), f32[32,1,1024]{2,1,0:T(1,128)S(1)}, u32[]{:S(2)}, u32[]{:S(2)}) async-start(f32[32,1,1024]{2,1,0:T(1,128)} %reshape.216), calls=%async_computation.8 | async-start | bytes 262144 | tf_op jit(solution)/shard_map/all_to_all | solution.py:22
  148.7 0.6 fusion.2
  149.9 9.0 %all-to-all-done.8 = f32[32,1,1024]{2,1,0:T(1,128)S(1)} async-done(((f32[32,1,1024]{2,1,0:T(1,128)}), f32[32,1,1024]{2,1,0:T(1,128)S(1)}, u32[]{:S(2)}, u32[]{:S(2)}) %all-to-all-start.8) | async-done | bytes 131104 | tf_op jit(solution)/shard_map/all_to_all | solution.py:22
  158.9 1.1 broadcast_in_dim.34
  160.0 3.5 all-to-all-start.7
  163.6 0.6 broadcast.126
  164.1 0.9 reduce.11
  165.4 2.9 cholesky.70
  168.3 4.8 %all-to-all-done.7 = f32[8,1,17408]{2,1,0:T(1,128)S(1)} async-done(((f32[8,1,17408]{2,1,0:T(1,128)}), f32[8,1,17408]{2,1,0:T(1,128)S(1)}, u32[]{:S(2)}, u32[]{:S(2)}) %all-to-all-start.7) | async-done | bytes 557088 | tf_op jit(solution)/shard_map/all_to_all | solution.py:22
  173.2 0.4 reduce_sum.84
  173.8 2.9 cholesky.59
  176.8 0.6 compare_reduce_fusion.2
  177.4 0.7 fusion.19
  178.1 2.4 custom-call.9
  181.7 0.9 reshape.218
  182.6 5.2 %all-to-all-start.9 = ((f32[32,1,1024]{2,1,0:T(1,128)}), f32[32,1,1024]{2,1,0:T(1,128)S(1)}, u32[]{:S(2)}, u32[]{:S(2)}) async-start(f32[32,1,1024]{2,1,0:T(1,128)} %reshape.218), calls=%async_computation.9 | async-start | bytes 262144 | tf_op jit(solution)/shard_map/all_to_all | solution.py:22
  187.8 0.6 compare_reduce_fusion.1
  188.5 0.7 fusion.20
  189.1 2.4 custom-call.10
  191.6 7.0 %all-to-all-done.9 = f32[32,1,1024]{2,1,0:T(1,128)S(1)} async-done(((f32[32,1,1024]{2,1,0:T(1,128)}), f32[32,1,1024]{2,1,0:T(1,128)S(1)}, u32[]{:S(2)}, u32[]{:S(2)}) %all-to-all-start.9) | async-done | bytes 131104 | tf_op jit(solution)/shard_map/all_to_all | solution.py:22
  198.6 0.9 reduce.12
  201.7 14.7 %all_to_all.97 = f32[32,1,1056]{2,1,0:T(1,128)S(1)} all-to-all(f32[32,1,1056]{2,1,0:T(1,128)S(1)} %all_to_all.71), channel_id=1, replica_groups=mesh['tp_0'=4,'tp_1'=2,'ex'=8,'co'=4] {'tp_0','tp_1','co'}, dimensions={0} | all-to-all | bytes 270336 | tf_op jit(solution)/shard_map/all_to_all | solution.py:38
  216.6 14.8 %all_to_all.98 = f32[32,1,1056]{2,1,0:T(1,128)S(1)} all-to-all(f32[32,1,1056]{2,1,0:T(1,128)S(1)} %broadcast_in_dim.37), channel_id=1, replica_groups=mesh['tp_0'=4,'tp_1'=2,'ex'=8,'co'=4] {'tp_0','tp_1','co'}, dimensions={0} | all-to-all | bytes 270336 | tf_op jit(solution)/shard_map/all_to_all | solution.py:22
  231.9 0.6 fusion.4
  233.1 1.1 broadcast_in_dim.38
  234.2 3.5 all-to-all-start.12
  238.0 9.3 %all-to-all-done.12 = f32[8,1,17408]{2,1,0:T(1,128)S(1)} async-done(((f32[8,1,17408]{2,1,0:T(1,128)}), f32[8,1,17408]{2,1,0:T(1,128)S(1)}, u32[]{:S(2)}, u32[]{:S(2)}) %all-to-all-start.12) | async-done | bytes 557088 | tf_op jit(solution)/shard_map/all_to_all | solution.py:22
  248.0 2.9 cholesky.81
  250.9 0.6 compare_reduce_fusion
  251.6 0.7 fusion.21
  252.2 2.4 custom-call.11
  256.5 15.2 %all_to_all.99 = f32[32,1,1024]{2,1,0:T(1,128)S(1)} all-to-all(f32[32,1,1024]{2,1,0:T(1,128)S(1)} %reshape.220), channel_id=1, replica_groups=mesh['tp_0'=4,'tp_1'=2,'ex'=8,'co'=4] {'tp_0','tp_1','co'}, dimensions={0} | all-to-all | bytes 262144 | tf_op jit(solution)/shard_map/all_to_all | solution.py:38
  271.7 0.9 reduce.13
  272.9 0.9 reshape.222
  273.8 4.2 %all-to-all-start.14 = ((f32[32,1,1024]{2,1,0:T(1,128)}), f32[32,1,1024]{2,1,0:T(1,128)S(1)}, u32[]{:S(2)}, u32[]{:S(2)}) async-start(f32[32,1,1024]{2,1,0:T(1,128)} %reshape.222), calls=%async_computation.14 | async-start | bytes 262144 | tf_op jit(solution)/shard_map/all_to_all | solution.py:22
  278.1 10.7 %all-to-all-done.14 = f32[32,1,1024]{2,1,0:T(1,128)S(1)} async-done(((f32[32,1,1024]{2,1,0:T(1,128)}), f32[32,1,1024]{2,1,0:T(1,128)S(1)}, u32[]{:S(2)}, u32[]{:S(2)}) %all-to-all-start.14) | async-done | bytes 131104 | tf_op jit(solution)/shard_map/all_to_all | solution.py:22
  288.8 0.9 reduce.14
  290.5 0.7 pad_maximum_fusion
  291.2 31.5 %all-gather.2.cloned.1.call-done = f32[8192,33]{0,1:T(8,128)} async-done(((f32[1024,33]{0,1:T(8,128)}), f32[8192,33]{0,1:T(8,128)}) %all-gather.2.cloned.1.call-update) | async-done | bytes 1081360 | tf_op jit(solution)/shard_map/all_gather | solution.py:121
  322.8 1.3 slice.102
  324.1 2.6 copy.118
  326.7 1.0 compare_select_fusion
  327.7 21.0 %scatter_custom_fusion = f32[1024,32]{1,0:T(8,128)S(1)} fusion(s32[8192]{0:T(1024)S(1)} %bitcast.121, f32[8192,32]{1,0:T(8,128)} %copy.118, f32[]{:T(128)} %constant.64.clone.1), kind=kCustom, calls=%fused_computation.21 | custom fusion | bytes 131584 | tf_op jit(solution)/shard_map/scatter | solution.py:234
  348.7 0.8 copy.119
  (115 shorter events, 13.6 us)
Async XLA Ops:
  7.2 103.4 %copy-start = (bf16[1024,512]{1,0:T(8,128)(2,1)S(1)}, bf16[1024,512]{1,0:T(8,128)(2,1)}, u32[]{:S(2)}) copy-start(bf16[1024,512]{1,0:T(8,128)(2,1)} %param.19) | copy-start | bytes 3145732
  8.9 9.7 %copy-start.4 = (bf16[448,128]{1,0:T(8,128)(2,1)S(1)}, bf16[448,128]{1,0:T(8,128)(2,1)}, u32[]{:S(2)}) copy-start(bf16[448,128]{1,0:T(8,128)(2,1)} %param.17) | copy-start | bytes 344068
  29.1 54.5 %copy-start.2 = (s32[1024]{0:T(1024)S(1)}, s32[1024]{0:T(1024)}, u32[]{:S(2)}) copy-start(s32[1024]{0:T(1024)} %param.14) | copy-start | bytes 12292
  76.5 22.0 %all-to-all-start.3 = ((f32[8,4,8192]{2,1,0:T(4,128)}), f32[8,4,8192]{2,1,0:T(4,128)S(1)}, u32[]{:S(2)}, u32[]{:S(2)}) async-start(f32[8,4,8192]{2,1,0:T(4,128)} %broadcast_in_dim.30), calls=%async_computation.3 | async-start | bytes 2097152 | tf_op jit(solution)/shard_map/all_to_all | solution.py:22
  128.6 15.3 %all-to-all-start.6 = ((f32[32,1,1056]{2,1,0:T(1,128)}), f32[32,1,1056]{2,1,0:T(1,128)S(1)}, u32[]{:S(2)}, u32[]{:S(2)}) async-start(f32[32,1,1056]{2,1,0:T(1,128)} %broadcast_in_dim.33), calls=%async_computation.6 | async-start | bytes 294912 | tf_op jit(solution)/shard_map/all_to_all | solution.py:22
  143.9 15.1 %all-to-all-start.8 = ((f32[32,1,1024]{2,1,0:T(1,128)}), f32[32,1,1024]{2,1,0:T(1,128)S(1)}, u32[]{:S(2)}, u32[]{:S(2)}) async-start(f32[32,1,1024]{2,1,0:T(1,128)} %reshape.216), calls=%async_computation.8 | async-start | bytes 262144 | tf_op jit(solution)/shard_map/all_to_all | solution.py:22
  160.0 13.2 %all-to-all-start.7 = ((f32[8,1,17408]{2,1,0:T(1,128)}), f32[8,1,17408]{2,1,0:T(1,128)S(1)}, u32[]{:S(2)}, u32[]{:S(2)}) async-start(f32[8,1,17408]{2,1,0:T(1,128)} %broadcast_in_dim.34), calls=%async_computation.7 | async-start | bytes 1114112 | tf_op jit(solution)/shard_map/all_to_all | solution.py:22
  182.6 16.0 %all-to-all-start.9 = ((f32[32,1,1024]{2,1,0:T(1,128)}), f32[32,1,1024]{2,1,0:T(1,128)S(1)}, u32[]{:S(2)}, u32[]{:S(2)}) async-start(f32[32,1,1024]{2,1,0:T(1,128)} %reshape.218), calls=%async_computation.9 | async-start | bytes 262144 | tf_op jit(solution)/shard_map/all_to_all | solution.py:22
  234.2 13.1 %all-to-all-start.12 = ((f32[8,1,17408]{2,1,0:T(1,128)}), f32[8,1,17408]{2,1,0:T(1,128)S(1)}, u32[]{:S(2)}, u32[]{:S(2)}) async-start(f32[8,1,17408]{2,1,0:T(1,128)} %broadcast_in_dim.38), calls=%async_computation.12 | async-start | bytes 1114112 | tf_op jit(solution)/shard_map/all_to_all | solution.py:22
  247.8 30.3 %copy-start.3 = (s32[1024]{0:T(1024)S(1)}, s32[1024]{0:T(1024)}, u32[]{:S(2)}) copy-start(s32[1024]{0:T(1024)} %param.20) | copy-start | bytes 12292
  255.3 34.6 %copy-start.1 = (f32[512,32]{0,1:T(8,128)}, f32[512,32]{0,1:T(8,128)S(1)}, u32[]{:S(2)}) copy-start(f32[512,32]{0,1:T(8,128)S(1)} %convolution_add_fusion) | copy-start | bytes 196612
  273.8 15.0 %all-to-all-start.14 = ((f32[32,1,1024]{2,1,0:T(1,128)}), f32[32,1,1024]{2,1,0:T(1,128)S(1)}, u32[]{:S(2)}, u32[]{:S(2)}) async-start(f32[32,1,1024]{2,1,0:T(1,128)} %reshape.222), calls=%async_computation.14 | async-start | bytes 262144 | tf_op jit(solution)/shard_map/all_to_all | solution.py:22
  278.0 44.7 %all-gather.2.cloned.1.call-start = ((), (), s32[]{:S(2)}) async-start(), calls=%async_computation.15 | async-start | bytes 1474560 | tf_op jit(solution)/shard_map/all_gather | solution.py:121
Sparse Core Ops, SparseCore 0:
  291.4 31.3 all-gather.1
where the time goes:
time: 362 us; the launch traced here: 356 us
  blocking collectives  116 us (32%)
  waiting for transfers between devices  97.4 us (27%)
  local copies, waits for them, and re-layouts  41.2 us (11%)
  starting transfers between devices  32.2 us (9%)
  other arithmetic  28.4 us (8%)
  matrix products  26.4 us (7%)
  between operations  14.7 us (4%)
    all_to_all x4, blocking collectives, sent_and_summed(): lax.all_to_all(split_up(value, dim, devices), axis, 0, 0, tiled=True)  66.6 us
    all_to_all x7, waiting for transfers between devices, from_everyone(): lax.all_to_all(jnp.broadcast_to(value[None], (devices, *value.shape)), ax...  65.8 us
    all_to_all x3, blocking collectives, from_everyone(): lax.all_to_all(jnp.broadcast_to(value[None], (devices, *value.shape)), ax...  34.3 us
    all_to_all x7, starting transfers between devices, from_everyone(): lax.all_to_all(jnp.broadcast_to(value[None], (devices, *value.shape)), ax...  32.1 us
    all_gather x1, waiting for transfers between devices, in_one_piece(): whole, at, outs = (lax.all_gather(both, axis, axis=dim, tiled=True), 0, [])  31.5 us
    scatter x1, local copies, waits for them, and re-layouts, local(): placed = jnp.zeros((rows_local, all_scores.shape[1]), jnp.float32).at[pos...  21 us
    all_to_all x1, blocking collectives, sum_by_axis(): lax.all_to_all(nearer, far, split_axis=0, concat_axis=0, tiled=True)  15.2 us
    another operation x9, other arithmetic, solve_spd(): factor = jnp.linalg.cholesky(matrix)  10.8 us
  transfers between devices with their start and end apart: 8, of which 8 were waited for; matrix products, arithmetic and copies ran while one was open for 3% of the time, Pallas kernels for 0%

commit v1 on v0

--- a/solution.py
+++ b/solution.py
@@ -195,35 +195,32 @@
     targets = gather_directly(local_grads, "ex", 1)
     rows_local = database.shape[0]
     gram_scale = 1.0 / math.sqrt(float(rows_local * ex_count))
-    solution = jnp.zeros_like(targets)
-    residual = targets
-    direction = targets
-    norm_now = residual_gram(residual)
-    for step_index in range(ITERS):
-        packed = direction.astype(jnp.bfloat16)
-        partial_rows = jnp.dot(database, packed, preferred_element_type=jnp.float32)
-        row_sums, direction_gram = in_one_2((partial_rows, inner_gram(direction, direction)), TP_CO)
-        scaled_rows = row_sums * gram_scale
-        rows_low = scaled_rows.astype(jnp.bfloat16)
-        back_term = lax.dot_general(
-            database, rows_low, (((0,), (0,)), ((), ())), preferred_element_type=jnp.float32
-        )
-        back_sum, rows_gram = together(
-            (back_term, inner_gram(scaled_rows, rows_low.astype(jnp.float32))), "ex"
-        )
-        image = back_sum * gram_scale + DAMPING * direction
-        curvature = symmetric(rows_gram + DAMPING * direction_gram)
-        step_size = solve_spd(curvature, norm_now)
-        solution = solution + times_small(direction, step_size)
-        residual = residual - times_small(image, step_size)
-        if step_index + 1 < ITERS:
-            norm_next = residual_gram(residual)
-            mixing = solve_spd(norm_now, norm_next)
-            direction = residual + times_small(direction, mixing)
-            norm_now = norm_next
-    final_low = solution.astype(jnp.bfloat16)
-    score_part = jnp.dot(database, final_low, preferred_element_type=jnp.float32)
-    score_rows = total_of(score_part, TP_CO) * (1.0 / math.sqrt(K))
+    packed = targets.astype(jnp.bfloat16)
+    rows_part = jnp.dot(database, packed, preferred_element_type=jnp.float32)
+    rows0, norm0 = in_one_2((rows_part, inner_gram(targets, targets)), TP_CO)
+    low0 = (rows0 * gram_scale).astype(jnp.bfloat16)
+    back_term = lax.dot_general(
+        database, low0, (((0,), (0,)), ((), ())), preferred_element_type=jnp.float32
+    )
+    back_sum, rows_gram = together((back_term, inner_gram(rows0, rows0)), "ex")
+    image = back_sum * gram_scale + DAMPING * targets
+    step0 = solve_spd(rows_gram * gram_scale**2 + DAMPING * norm0, norm0)
+    residual = targets - times_small(image, step0)
+    rows_part = jnp.dot(
+        database, residual.astype(jnp.bfloat16), preferred_element_type=jnp.float32
+    )
+    rows_r, norm1, cross = in_one_2(
+        (rows_part, inner_gram(residual, residual), inner_gram(targets, residual)), TP_CO
+    )
+    mixing = solve_spd(norm0, norm1)
+    rows1 = rows_r + times_small(rows0, mixing)
+    mixed = inner_gram(mixing, cross)
+    gram1 = norm1 + mixed + mixed.T + inner_gram(mixing, times_small(norm0, mixing))
+    (rows_gram1,) = together((inner_gram(rows1, rows1),), "ex")
+    step1 = solve_spd(symmetric(rows_gram1 * gram_scale**2 + DAMPING * gram1), norm1)
+    direction = residual + times_small(targets, mixing)
+    solution = times_small(targets, step0) + times_small(direction, step1)
+    score_rows = (times_small(rows0, step0) + times_small(rows1, step1)) * (1.0 / math.sqrt(K))
     all_scores, all_ids = in_one_piece((score_rows, stored_ids.astype(jnp.float32)), "ex", 0, 1)
     position = all_ids.astype(jnp.int32) - ex_index * rows_local
     inside = (position >= 0) & (position < rows_local)

time: 362 us -> 294 us (0.81)
  blocking collectives: 116 us -> 86.2 us
  waiting for transfers between devices: 97.4 us -> 76 us
  starting transfers between devices: 32.2 us -> 23.8 us
  local copies, waits for them, and re-layouts: 41.2 us -> 36.1 us
  other arithmetic: 28.4 us -> 24 us
    all_to_all x4 -> x2, blocking collectives: 66.6 us -> 36.7 us  [sent_and_summed(): lax.all_to_all(split_up(value, dim, devices), axis, 0, 0, tiled=True)]
    all_to_all x7 -> x4, waiting for transfers between devices: 65.8 us -> 36.2 us  [from_everyone(): lax.all_to_all(jnp.broadcast_to(value[None], (devices, *value.shape)), ax...]
    all_to_all x7 -> x4, starting transfers between devices: 32.1 us -> 18.2 us  [from_everyone(): lax.all_to_all(jnp.broadcast_to(value[None], (devices, *value.shape)), ax...]
    all_to_all x0 -> x1, waiting for transfers between devices: none -> 8.05 us  [sent_and_summed(): lax.all_to_all(split_up(value, dim, devices), axis, 0, 0, tiled=True)]
    all_to_all x0 -> x1, starting transfers between devices: none -> 5.3 us  [sent_and_summed(): lax.all_to_all(split_up(value, dim, devices), axis, 0, 0, tiled=True)]
  transfers between devices with their start and end apart: 8 -> 6, of which waited for: 8 -> 6; matrix products, arithmetic and copies ran while one was open for 3% -> 3% of each run, Pallas kernels for 0% -> 0%
where the time goes in v1:
time: 294 us; the launch traced here: 289 us
  blocking collectives  86.2 us (29%)
  waiting for transfers between devices  76 us (26%)
  local copies, waits for them, and re-layouts  36.1 us (12%)
  matrix products  28.7 us (10%)
  other arithmetic  24 us (8%)
  starting transfers between devices  23.8 us (8%)
  between operations  14.6 us (5%)
    all_to_all x2, blocking collectives, sent_and_summed(): lax.all_to_all(split_up(value, dim, devices), axis, 0, 0, tiled=True)  36.7 us
    all_to_all x4, waiting for transfers between devices, from_everyone(): lax.all_to_all(jnp.broadcast_to(value[None], (devices, *value.shape)), ax...  36.2 us
    all_to_all x3, blocking collectives, from_everyone(): lax.all_to_all(jnp.broadcast_to(value[None], (devices, *value.shape)), ax...  34.3 us
    all_gather x1, waiting for transfers between devices, in_one_piece(): whole, at, outs = (lax.all_gather(both, axis, axis=dim, tiled=True), 0, [])  31.8 us
    scatter x1, local copies, waits for them, and re-layouts, local(): placed = jnp.zeros((rows_local, all_scores.shape[1]), jnp.float32).at[pos...  21 us
    all_to_all x4, starting transfers between devices, from_everyone(): lax.all_to_all(jnp.broadcast_to(value[None], (devices, *value.shape)), ax...  18.2 us
    all_to_all x1, blocking collectives, sum_by_axis(): lax.all_to_all(nearer, far, split_axis=0, concat_axis=0, tiled=True)  15.2 us
    another operation x9, other arithmetic, solve_spd(): factor = jnp.linalg.cholesky(matrix)  10.8 us
  transfers between devices with their start and end apart: 6, of which 6 were waited for; matrix products, arithmetic and copies ran while one was open for 3% of the time, Pallas kernels for 0%

profile of v1, /device:TPU:1, one launch (start us, length us, event | category | flops | bytes accessed | tf_op | source)
XLA Modules:
  0.0 289.4 jit_solution(17641381563424405789)
XLA Ops:
  7.2 1.2 fusion.46
  8.5 0.4 copy.89
  9.0 9.7 %fusion.45 = f32[1024,448]{0,1:T(8,128)} fusion(bf16[1024,4096]{1,0:T(8,128)(2,1)} %param.12, bf16[4096,448]{0,1:T(8,128)(2,1)} %param.15), kind=kOutput, calls=%fused_computation.90 | convolution fusion | flops 3758096384 | bytes 13893632 | tf_op jit(solution)/shard_map/dot_general | solution.py:188
  18.7 9.4 %fusion = f32[1024,128]{1,0:T(8,128)S(1)} fusion(bf16[448,128]{1,0:T(8,128)(2,1)S(1)} %copy-done.3, f32[1024,448]{0,1:T(8,128)} %fusion.45, bf16[1024,4096]{1,0:T(8,128)(2,1)} %param.12, bf16[4096,448]{0,1:T(8,128)(2,1)} %param.16), kind=kOutput, calls=%fused_computation.2 | convolution fusion | flops 3878289408 | bytes 14532608 | tf_op jit(solution)/shard_map/dot_general | solution.py:191
  28.2 0.4 copy.88
  28.6 0.5 maximum_bitcast_fusion
  29.1 20.6 %all_to_all.72 = f32[8,4,8192]{2,1,0:T(4,128)S(1)} all-to-all(f32[8,4,8192]{2,1,0:T(4,128)S(1)} %maximum_bitcast_fusion), channel_id=1, replica_groups=mesh['tp_0'=4,'tp_1'=2,'ex'=8,'co'=4] {'tp_1','co'}, dimensions={0} | all-to-all | bytes 2097152 | tf_op jit(solution)/shard_map/all_to_all | solution.py:38
  50.0 15.2 %all_to_all.73 = f32[4,1,8192]{2,1,0:T(1,128)S(1)} all-to-all(f32[4,1,8192]{2,1,0:T(1,128)S(1)} %all_to_all.48), channel_id=1, replica_groups=mesh['tp_0'=4,'tp_1'=2,'ex'=8,'co'=4] {'tp_0'}, dimensions={0} | all-to-all | bytes 262144 | tf_op jit(solution)/shard_map/all_to_all | solution.py:46
  65.4 9.9 %all_to_all.74 = f32[4,1,8192]{2,1,0:T(1,128)S(1)} all-to-all(f32[4,1,8192]{2,1,0:T(1,128)S(1)} %broadcast_in_dim.23), channel_id=1, replica_groups=mesh['tp_0'=4,'tp_1'=2,'ex'=8,'co'=4] {'tp_0'}, dimensions={0} | all-to-all | bytes 262144 | tf_op jit(solution)/shard_map/all_to_all | solution.py:22
  75.4 1.1 broadcast_in_dim.26
  76.5 7.0 %all-to-all-start.3 = ((f32[8,4,8192]{2,1,0:T(4,128)}), f32[8,4,8192]{2,1,0:T(4,128)S(1)}, u32[]{:S(2)}, u32[]{:S(2)}) async-start(f32[8,4,8192]{2,1,0:T(4,128)} %broadcast_in_dim.26), calls=%async_computation.3 | async-start | bytes 2097152 | tf_op jit(solution)/shard_map/all_to_all | solution.py:22
  83.6 15.0 %all-to-all-done.3 = f32[8,4,8192]{2,1,0:T(4,128)S(1)} async-done(((f32[8,4,8192]{2,1,0:T(4,128)}), f32[8,4,8192]{2,1,0:T(4,128)S(1)}, u32[]{:S(2)}, u32[]{:S(2)}) %all-to-all-start.3) | async-done | bytes 1048608 | tf_op jit(solution)/shard_map/all_to_all | solution.py:22
  98.5 0.4 fusion.44
  98.9 0.3 copy.92
  99.3 0.3 copy.90
  100.2 0.4 convolution_bitcast_fusion.3
  100.7 9.6 %all_to_all.75 = f32[8,512,4]{1,2,0:T(4,128)S(1)} all-to-all(f32[8,512,4]{1,2,0:T(4,128)S(1)} %broadcast_in_dim.28), channel_id=1, replica_groups=mesh['tp_0'=4,'tp_1'=2,'ex'=8,'co'=4] {'ex'}, dimensions={0} | all-to-all | bytes 131072 | tf_op jit(solution)/shard_map/all_to_all | solution.py:22
  110.5 0.4 convolution_bitcast_fusion.1
  111.6 16.1 %all_to_all.76 = f32[32,1,1056]{2,1,0:T(1,128)S(1)} all-to-all(f32[32,1,1056]{2,1,0:T(1,128)S(1)} %all_to_all.53), channel_id=1, replica_groups=mesh['tp_0'=4,'tp_1'=2,'ex'=8,'co'=4] {'tp_0','tp_1','co'}, dimensions={0} | all-to-all | bytes 270336 | tf_op jit(solution)/shard_map/all_to_all | solution.py:38
  127.9 14.8 %all_to_all.77 = f32[32,1,1056]{2,1,0:T(1,128)S(1)} all-to-all(f32[32,1,1056]{2,1,0:T(1,128)S(1)} %broadcast_in_dim.29), channel_id=1, replica_groups=mesh['tp_0'=4,'tp_1'=2,'ex'=8,'co'=4] {'tp_0','tp_1','co'}, dimensions={0} | all-to-all | bytes 270336 | tf_op jit(solution)/shard_map/all_to_all | solution.py:22
  142.7 0.4 reduce.9
  143.2 1.0 fusion.6
  144.2 0.3 convolution_bitcast_fusion.2
  144.9 1.1 broadcast_in_dim.30
  146.0 3.5 %all-to-all-start.7 = ((f32[8,1,17408]{2,1,0:T(1,128)}), f32[8,1,17408]{2,1,0:T(1,128)S(1)}, u32[]{:S(2)}, u32[]{:S(2)}) async-start(f32[8,1,17408]{2,1,0:T(1,128)} %broadcast_in_dim.30), calls=%async_computation.7 | async-start | bytes 1114112 | tf_op jit(solution)/shard_map/all_to_all | solution.py:22
  149.6 9.4 %all-to-all-done.7 = f32[8,1,17408]{2,1,0:T(1,128)S(1)} async-done(((f32[8,1,17408]{2,1,0:T(1,128)}), f32[8,1,17408]{2,1,0:T(1,128)S(1)}, u32[]{:S(2)}, u32[]{:S(2)}) %all-to-all-start.7) | async-done | bytes 557088 | tf_op jit(solution)/shard_map/all_to_all | solution.py:22
  159.1 0.4 reduce_sum.57
  159.7 2.9 %cholesky.59 = f32[32,32]{1,0:T(8,128)S(1)} custom-call(f32[32,32]{1,0:T(8,128)S(1)} %fusion.35), custom_call_target="Cholesky" | custom-call | tf_op jit(solution)/shard_map/jit(cholesky)/cholesky | solution.py:144
  162.7 0.6 compare_reduce_fusion.2
  163.3 0.7 fusion.15
  164.0 2.4 custom-call.9
  167.0 0.3 convolution_subtract_fusion
  167.7 0.4 convolution_bitcast_fusion
  168.7 0.8 all_to_all.57
  169.5 5.3 %all-to-all-start.8 = ((f32[32,1,1088]{2,1,0:T(1,128)}), f32[32,1,1088]{2,1,0:T(1,128)S(1)}, u32[]{:S(2)}, u32[]{:S(2)}) async-start(f32[32,1,1088]{2,1,0:T(1,128)} %all_to_all.57), calls=%async_computation.8 | async-start | bytes 294912 | tf_op jit(solution)/shard_map/all_to_all | solution.py:38
  174.8 2.9 %cholesky.70 = f32[32,32]{1,0:T(8,128)S(1)} custom-call(f32[32,32]{1,0:T(8,128)S(1)} %fusion.30), custom_call_target="Cholesky" | custom-call | tf_op jit(solution)/shard_map/jit(cholesky)/cholesky | solution.py:144
  177.8 8.0 %all-to-all-done.8 = f32[32,1,1088]{2,1,0:T(1,128)S(1)} async-done(((f32[32,1,1088]{2,1,0:T(1,128)}), f32[32,1,1088]{2,1,0:T(1,128)S(1)}, u32[]{:S(2)}, u32[]{:S(2)}) %all-to-all-start.8) | async-done | bytes 139296 | tf_op jit(solution)/shard_map/all_to_all | solution.py:38
  185.9 0.7 broadcast_in_dim.31
  186.7 4.3 %all-to-all-start.9 = ((f32[32,1,1088]{2,1,0:T(1,128)}), f32[32,1,1088]{2,1,0:T(1,128)S(1)}, u32[]{:S(2)}, u32[]{:S(2)}) async-start(f32[32,1,1088]{2,1,0:T(1,128)} %broadcast_in_dim.31), calls=%async_computation.9 | async-start | bytes 294912 | tf_op jit(solution)/shard_map/all_to_all | solution.py:22
  191.0 0.6 compare_reduce_fusion.1
  191.6 0.7 fusion.16
  192.3 2.4 custom-call.10
  194.7 7.2 %all-to-all-done.9 = f32[32,1,1088]{2,1,0:T(1,128)S(1)} async-done(((f32[32,1,1088]{2,1,0:T(1,128)}), f32[32,1,1088]{2,1,0:T(1,128)S(1)}, u32[]{:S(2)}, u32[]{:S(2)}) %all-to-all-start.9) | async-done | bytes 139296 | tf_op jit(solution)/shard_map/all_to_all | solution.py:22
  201.9 0.4 reduce.10
  203.3 0.7 convolution_add_fusion.1
  204.3 0.6 broadcast_in_dim.33
  204.9 3.3 %all-to-all-start.10 = ((f32[8,1,1024]{2,1,0:T(1,128)}), f32[8,1,1024]{2,1,0:T(1,128)S(1)}, u32[]{:S(2)}, u32[]{:S(2)}) async-start(f32[8,1,1024]{2,1,0:T(1,128)} %broadcast_in_dim.33), calls=%async_computation.10 | async-start | bytes 65536 | tf_op jit(solution)/shard_map/all_to_all | solution.py:22
  208.3 0.3 all-gather.2.cloned.1.call-start
  208.7 4.6 %all-to-all-done.10 = f32[8,1,1024]{2,1,0:T(1,128)S(1)} async-done(((f32[8,1,1024]{2,1,0:T(1,128)}), f32[8,1,1024]{2,1,0:T(1,128)S(1)}, u32[]{:S(2)}, u32[]{:S(2)}) %all-to-all-start.10) | async-done | bytes 32800 | tf_op jit(solution)/shard_map/all_to_all | solution.py:22
  213.8 2.9 %cholesky.81 = f32[32,32]{1,0:T(8,128)S(1)} custom-call(f32[32,32]{1,0:T(8,128)S(1)} %fusion.24), custom_call_target="Cholesky" | custom-call | tf_op jit(solution)/shard_map/jit(cholesky)/cholesky | solution.py:144
  216.8 0.6 compare_reduce_fusion
  217.4 0.7 fusion.17
  218.1 2.4 custom-call.11
  220.9 0.3 fusion.52
  221.2 0.7 fusion.1
  221.9 0.7 pad_maximum_fusion
  222.8 0.3 convolution_add_fusion.3
  223.1 0.9 convolution_add_fusion.2
  224.0 31.8 %all-gather.2.cloned.1.call-done = f32[8192,33]{0,1:T(8,128)} async-done(((f32[1024,33]{0,1:T(8,128)}), f32[8192,33]{0,1:T(8,128)}) %all-gather.2.cloned.1.call-update) | async-done | bytes 1081360 | tf_op jit(solution)/shard_map/all_gather | solution.py:121
  255.8 1.3 slice.95
  257.1 2.6 copy.109
  259.7 1.0 compare_select_fusion
  260.7 21.0 %scatter_custom_fusion = f32[1024,32]{1,0:T(8,128)S(1)} fusion(s32[8192]{0:T(1024)S(1)} %bitcast.108, f32[8192,32]{1,0:T(8,128)} %copy.109, f32[]{:T(128)} %constant.65.clone.1), kind=kCustom, calls=%fused_computation.22 | custom fusion | bytes 131584 | tf_op jit(solution)/shard_map/scatter | solution.py:231
  281.7 0.8 copy.110
  (87 shorter events, 7.6 us)
Async XLA Ops:
  7.2 103.4 %copy-start = (bf16[1024,512]{1,0:T(8,128)(2,1)S(1)}, bf16[1024,512]{1,0:T(8,128)(2,1)}, u32[]{:S(2)}) copy-start(bf16[1024,512]{1,0:T(8,128)(2,1)} %param.19) | copy-start | bytes 3145732
  8.9 9.7 %copy-start.3 = (bf16[448,128]{1,0:T(8,128)(2,1)S(1)}, bf16[448,128]{1,0:T(8,128)(2,1)}, u32[]{:S(2)}) copy-start(bf16[448,128]{1,0:T(8,128)(2,1)} %param.17) | copy-start | bytes 344068
  29.1 54.5 %copy-start.1 = (s32[1024]{0:T(1024)S(1)}, s32[1024]{0:T(1024)}, u32[]{:S(2)}) copy-start(s32[1024]{0:T(1024)} %param.14) | copy-start | bytes 12292
  76.5 22.0 %all-to-all-start.3 = ((f32[8,4,8192]{2,1,0:T(4,128)}), f32[8,4,8192]{2,1,0:T(4,128)S(1)}, u32[]{:S(2)}, u32[]{:S(2)}) async-start(f32[8,4,8192]{2,1,0:T(4,128)} %broadcast_in_dim.26), calls=%async_computation.3 | async-start | bytes 2097152 | tf_op jit(solution)/shard_map/all_to_all | solution.py:22
  111.3 38.2 %copy-start.2 = (s32[1024]{0:T(1024)S(1)}, s32[1024]{0:T(1024)}, u32[]{:S(2)}) copy-start(s32[1024]{0:T(1024)} %param.20) | copy-start | bytes 12292
  146.0 13.1 %all-to-all-start.7 = ((f32[8,1,17408]{2,1,0:T(1,128)}), f32[8,1,17408]{2,1,0:T(1,128)S(1)}, u32[]{:S(2)}, u32[]{:S(2)}) async-start(f32[8,1,17408]{2,1,0:T(1,128)} %broadcast_in_dim.30), calls=%async_computation.7 | async-start | bytes 1114112 | tf_op jit(solution)/shard_map/all_to_all | solution.py:22
  169.5 16.3 %all-to-all-start.8 = ((f32[32,1,1088]{2,1,0:T(1,128)}), f32[32,1,1088]{2,1,0:T(1,128)S(1)}, u32[]{:S(2)}, u32[]{:S(2)}) async-start(f32[32,1,1088]{2,1,0:T(1,128)} %all_to_all.57), calls=%async_computation.8 | async-start | bytes 294912 | tf_op jit(solution)/shard_map/all_to_all | solution.py:38
  186.7 15.3 %all-to-all-start.9 = ((f32[32,1,1088]{2,1,0:T(1,128)}), f32[32,1,1088]{2,1,0:T(1,128)S(1)}, u32[]{:S(2)}, u32[]{:S(2)}) async-start(f32[32,1,1088]{2,1,0:T(1,128)} %broadcast_in_dim.31), calls=%async_computation.9 | async-start | bytes 294912 | tf_op jit(solution)/shard_map/all_to_all | solution.py:22
  204.9 8.4 %all-to-all-start.10 = ((f32[8,1,1024]{2,1,0:T(1,128)}), f32[8,1,1024]{2,1,0:T(1,128)S(1)}, u32[]{:S(2)}, u32[]{:S(2)}) async-start(f32[8,1,1024]{2,1,0:T(1,128)} %broadcast_in_dim.33), calls=%async_computation.10 | async-start | bytes 65536 | tf_op jit(solution)/shard_map/all_to_all | solution.py:22
  208.3 47.5 %all-gather.2.cloned.1.call-start = ((), (), s32[]{:S(2)}) async-start(), calls=%async_computation.11 | async-start | bytes 1474560 | tf_op jit(solution)/shard_map/all_gather | solution.py:121
Sparse Core Ops, SparseCore 0:
  222.7 33.0 all-gather.1

commit v2 on v1

v2 whole, which is shorter than its diff:
```python
import functools
import math

import jax
import jax.numpy as jnp
from jax import lax
from jax.experimental import pallas as pl
from jax.experimental.pallas import tpu as pltpu
from jax.sharding import PartitionSpec as P

D = 4096
FFL = 448
TOK = 1024
CHUNK = 256
CHUNKS = TOK // CHUNK
KB = 512
KSTEPS = D // KB
R = 128
Q = 32
QPG = 4
COORDS = 512
ROWS = 1024
EX = 8
GROUP = 8
ZH = 4
K = 16384
NSTORE = 8192
DAMPING = 1.0
HIGHEST = lax.Precision.HIGHEST
MESH = pl.DeviceIdType.MESH
F32 = jnp.float32
BF16 = jnp.bfloat16

PHASES = (
    ["ids", "r1", "r2", "r3"]
    + [f"l1{c}" for c in range(CHUNKS)]
    + [f"l2{c}" for c in range(CHUNKS)]
    + ["b", "y10", "y20", "y30", "z1", "z3", "s0", "y11", "y21", "y31", "s1", "c1"]
)
PHASE = {name: at for at, name in enumerate(PHASES)}


def fdot(a, b, dims=((1,), (0,))):
    return lax.dot_general(a, b, (dims, ((), ())), precision=HIGHEST, preferred_element_type=F32)


def bdot(a, b, dims=((1,), (0,))):
    return lax.dot_general(a, b, (dims, ((), ())), preferred_element_type=F32)


TN = ((0,), (0,))
NT = ((1,), (1,))


def eliminated(matrix, target):
    n = matrix.shape[0]
    both = jnp.concatenate([matrix, target], axis=1)
    lines = lax.broadcasted_iota(jnp.int32, both.shape, 0)
    for k in range(n):
        row = both[k : k + 1, :] / both[k : k + 1, k : k + 1]
        both = jnp.where(lines == k, row, both - both[:, k : k + 1] * row)
    return both[:, n:]


def kernel(
    q_hbm, cot_hbm, qot_hbm, gw_hbm, uw_hbm, pin_hbm, pout_hbm, db_hbm, ids_hbm,
    sol_ref, score_ref,
    q_v, cot_v, qot_v, gw_v, uw_v, pin_v, pout_v, db_v,
    acc_g, acc_u,
    ids_all, rsend, r1, r2, right,
    lsend, l1, l2,
    bbuf,
    ysend, y1, y2, yfull,
    zsend, z1, zfull,
    cbuf, s0, s1, picked, where_v, where_s,
    small_sem, q_sem, w_sem, send_sem, recv_sem,
):
    tp = lax.axis_index("tp")
    e = lax.axis_index("ex")
    x = lax.axis_index("co")
    zh = tp // 2
    core = tp % 2
    g = core * 4 + x
    scale = 1.0 / math.sqrt(float(NSTORE))

    def in_group(p):
        return {"tp": zh * 2 + p // 4, "co": p % 4}

    def in_z(p):
        return {"tp": p * 2 + core}

    def in_ex(p):
        return {"ex": p}

    def push(phase, src_of, dst, me, n, device_of):
        at = PHASE[phase]
        for d in range(1, n):
            p = (me + d) % n
            pltpu.make_async_remote_copy(
                src_of(p), dst, send_sem.at[at], recv_sem.at[at], device_of(p), MESH
            ).start()

    def arrived(phase, slots):
        pltpu.make_async_copy(slots, slots, recv_sem.at[PHASE[phase]]).wait()

    def sent(phase, slots):
        pltpu.make_async_copy(slots, slots, send_sem.at[PHASE[phase]]).wait()

    copies = [
        pltpu.make_async_copy(cot_hbm, cot_v, small_sem.at[0]),
        pltpu.make_async_copy(pout_hbm, pout_v, small_sem.at[1]),
        pltpu.make_async_copy(ids_hbm, ids_all.at[e], small_sem.at[2]),
        pltpu.make_async_copy(qot_hbm, qot_v, small_sem.at[3]),
        pltpu.make_async_copy(pin_hbm, pin_v, small_sem.at[4]),
        pltpu.make_async_copy(db_hbm, db_v, small_sem.at[5]),
    ]

    def q_copy(c):
        rows = pl.ds(c * CHUNK, CHUNK)
        return pltpu.make_async_copy(q_hbm.at[rows, :], q_v.at[rows, :], q_sem.at[c])

    def w_copy(k, side):
        cols = pl.ds(pl.multiple_of(k * KB, KB), KB)
        src, dst = ((gw_hbm, gw_v), (uw_hbm, uw_v))[side]
        return pltpu.make_async_copy(src.at[:, cols], dst.at[:, cols], w_sem.at[side, k])

    copies[0].start()
    copies[1].start()
    copies[2].start()
    q_copy(0).start()
    for k in range(KSTEPS):
        w_copy(k, 0).start()
        w_copy(k, 1).start()
        if k == 1:
            copies[3].start()
            copies[4].start()
    for c in range(1, CHUNKS):
        q_copy(c).start()
    copies[5].start()

    barrier = pltpu.get_barrier_semaphore()
    for n, me, device_of in ((GROUP, g, in_group), (ZH, zh, in_z), (EX, e, in_ex)):
        for d in range(1, n):
            pl.semaphore_signal(
                barrier, inc=1, device_id=device_of((me + d) % n), device_id_type=MESH
            )

    copies[0].wait()
    copies[1].wait()
    rsend[...] = bdot(cot_v[...], pout_v[...]).reshape(GROUP, R, R)
    copies[2].wait()

    pl.semaphore_wait(barrier, (GROUP - 1) + (ZH - 1) + (EX - 1))
    push("ids", lambda p: ids_all.at[e], ids_all.at[e], e, EX, in_ex)
    push("r1", lambda p: rsend.at[p], r1.at[g], g, GROUP, in_group)
    r1[g] = rsend[g]

    def matmul(c, first):
        rows = pl.ds(c * CHUNK, CHUNK)
        q_copy(c).wait()
        acc_g[...] = jnp.zeros_like(acc_g)
        acc_u[...] = jnp.zeros_like(acc_u)

        def step(k, carry):
            if first:
                w_copy(k, 0).wait()
                w_copy(k, 1).wait()
            cols = pl.ds(pl.multiple_of(k * KB, KB), KB)
            a = q_v[rows, cols]
            acc_g[...] += bdot(gw_v[:, cols], a, NT)
            acc_u[...] += bdot(uw_v[:, cols], a, NT)
            return carry

        lax.fori_loop(0, KSTEPS, step, 0)
        gate = acc_g[...]
        hidden = ((gate / (1.0 + jnp.exp(-gate))) * acc_u[...]).astype(BF16)
        left = bdot(pin_v[...], hidden, TN)
        a, b = left[:, :R], left[:, R:]
        low = lax.broadcasted_iota(jnp.int32, (R, R), 0) % 8 < 4
        lsend[c, 0] = jnp.where(low, a, pltpu.roll(b, 4, 0)).reshape(ZH, 4, 8, R)
        lsend[c, 1] = jnp.where(low, pltpu.roll(a, R - 4, 0), b).reshape(ZH, 4, 8, R)
        push(
            f"l1{c}", lambda p: lsend.at[c, p % 2, :, p // 2], l1.at[c, g], g, GROUP, in_group
        )
        l1[c, g] = lsend[c, g % 2, :, g // 2]

    def left_second(c):
        arrived(f"l1{c}", l1.at[c, pl.ds(0, GROUP - 1)])
        total = l1[c, 0]
        for s in range(1, GROUP):
            total = total + l1[c, s]
        sent(f"l1{c}", l1.at[c, pl.ds(0, GROUP - 1)])
        lsend[c, 0, 0] = total
        l2[c, zh] = lsend[c, 0, 0, zh]
        push(f"l2{c}", lambda p: lsend.at[c, 0, 0, p], l2.at[c, zh], zh, ZH, in_z)

    for c in range(CHUNKS):
        if c == 0:
            copies[4].wait()
        matmul(c, c == 0)
        if c == 0:
            arrived("r1", r1.at[pl.ds(0, GROUP - 1)])
            sent("r1", r1.at[pl.ds(0, GROUP - 1)])
            total = r1[0]
            for s in range(1, GROUP):
                total = total + r1[s]
            r2[zh] = total
            push("r2", lambda p: r2.at[zh], r2.at[zh], zh, ZH, in_z)
        if c == 1:
            arrived("r2", r2.at[pl.ds(0, ZH - 1)])
            right[g] = r2[0] + r2[1] + r2[2] + r2[3]
            push("r3", lambda p: right.at[g], right.at[g], g, GROUP, in_group)
        if c > 0:
            left_second(c - 1)

    arrived("ids", ids_all.at[pl.ds(0, EX - 1)])
    kinds = lax.broadcasted_iota(jnp.int32, (Q, R), 0)
    lane = lax.broadcasted_iota(jnp.int32, (Q, R), 1)
    places = jnp.zeros((Q, 2 * Q), F32)
    for s in range(EX):
        his, los = [], []
        for r in range(8):
            own = ids_all[s, pl.ds(r, 1), :] - e * ROWS
            hit_low = (own & 31) == kinds
            part = s * 2 + r % 2 + 16 * (r // 2)
            his.append(jnp.where((own >> 5) == kinds, 1.0, 0.0).astype(BF16))
            los.append(
                jnp.concatenate(
                    [
                        jnp.where(hit_low, float(part), 0.0),
                        jnp.where(hit_low, lane.astype(F32), 0.0),
                    ],
                    axis=0,
                ).astype(BF16)
            )
        places = places + bdot(
            jnp.concatenate(his, axis=1), jnp.concatenate(los, axis=1), NT
        )
    part = places[:, :Q].astype(jnp.int32)
    at = (part & 15) * R + places[:, Q:].astype(jnp.int32)
    where_v[...] = jnp.concatenate([at, part >> 4, at, at], axis=1)
    to_scalar = pltpu.make_async_copy(where_v, where_s, small_sem.at[6])
    to_scalar.start()

    left_second(CHUNKS - 1)
    arrived("r3", right.at[pl.ds(0, GROUP - 1)])
    copies[3].wait()
    copies[5].wait()
    high = lax.broadcasted_iota(jnp.int32, (8, R), 0) >= 4
    pieces, queries = [], []
    local = qot_v[...] - e * QPG
    for c in range(CHUNKS):
        arrived(f"l2{c}", l2.at[c, pl.ds(0, ZH - 1)])
        tile = l2[c, 0] + l2[c, 1] + l2[c, 2] + l2[c, 3]
        pieces.append(jnp.where(high, 0.0, tile))
        pieces.append(jnp.where(high, tile, 0.0))
        queries.append(local[2 * c : 2 * c + 1, :])
        queries.append(local[2 * c + 1 : 2 * c + 2, :])
    left = jnp.concatenate(pieces, axis=1)
    query = jnp.concatenate(queries, axis=1)
    weighted = jnp.concatenate(
        [jnp.where(query == k, left, 0.0) for k in range(QPG)], axis=0
    )
    grads = fdot(weighted, right[...].reshape(TOK, R))
    grads = grads + pltpu.roll(grads, 28, 0)
    mine = jnp.concatenate(
        [
            jnp.where(high, pltpu.roll(grads[8:16], 4, 0), grads[0:8]),
            jnp.where(high, pltpu.roll(grads[24:32], 4, 0), grads[16:24]),
        ],
        axis=0,
    )
    own_rows = pl.ds(pl.multiple_of(e * 16, 16), 16)
    bbuf[own_rows, :] = mine
    push("b", lambda p: bbuf.at[own_rows, :], bbuf.at[own_rows, :], e, EX, in_ex)
    arrived("b", bbuf.at[pl.ds(0, 16 * (EX - 1)), :])
    base = jnp.concatenate([bbuf[pl.ds(i, Q, stride=4), :] for i in range(4)], axis=1)

    def reduced(k, vectors, gram):
        part = bdot(vectors.astype(BF16), db_v[...], NT)
        for p in range(GROUP):
            ysend[k, p, :Q] = part[:, p * R : (p + 1) * R]
            ysend[k, p, Q:] = gram
        push(f"y1{k}", lambda p: ysend.at[k, p], y1.at[k, g], g, GROUP, in_group)
        y1[k, g] = ysend[k, g]
        arrived(f"y1{k}", y1.at[k, pl.ds(0, GROUP - 1)])
        total = y1[k, 0]
        for s in range(1, GROUP):
            total = total + y1[k, s]
        y2[k, zh] = total
        push(f"y2{k}", lambda p: y2.at[k, zh], y2.at[k, zh], zh, ZH, in_z)
        arrived(f"y2{k}", y2.at[k, pl.ds(0, ZH - 1)])
        total = y2[k, 0] + y2[k, 1] + y2[k, 2] + y2[k, 3]
        yfull[k, g] = total[:Q]
        push(f"y3{k}", lambda p: yfull.at[k, g], yfull.at[k, g], g, GROUP, in_group)
        return total[Q:]

    def rows_of(k):
        arrived(f"y3{k}", yfull.at[k, pl.ds(0, GROUP - 1)])
        return [yfull[k, s] for s in range(GROUP)]

    def packed(blocks):
        tall = [
            jnp.concatenate([blocks[2 * i + h] for i in range(4)], axis=0).T for h in range(2)
        ]
        return jnp.concatenate(tall, axis=0)

    gram0 = reduced(0, base, fdot(base, jnp.concatenate([base] * 4, axis=0), NT))
    norm0 = gram0[:, :Q]
    eye = (
        lax.broadcasted_iota(jnp.int32, (Q, Q), 0) == lax.broadcasted_iota(jnp.int32, (Q, Q), 1)
    ).astype(F32)
    inverse0 = eliminated(norm0, eye)
    blocks0 = rows_of(0)
    rows0 = jnp.concatenate(blocks0, axis=1)

    back = bdot((rows0 * scale).astype(BF16), db_v[...])
    row_gram = fdot(rows0, jnp.concatenate([rows0] * 4, axis=0), NT)
    for p in range(EX):
        zsend[p, :16] = back[16 * (p // 4) : 16 * (p // 4) + 16, (p % 4) * R : (p % 4 + 1) * R]
        zsend[p, 16:] = row_gram
    push("z1", lambda p: zsend.at[p], z1.at[e], e, EX, in_ex)
    z1[e] = zsend[e]
    arrived("z1", z1.at[pl.ds(0, EX - 1)])
    total = z1[0]
    for s in range(1, EX):
        total = total + z1[s]
    zfull[e] = total[:16]
    push("z3", lambda p: zfull.at[e], zfull.at[e], e, EX, in_ex)
    step0 = eliminated(total[16:, :Q] * (scale * scale) + DAMPING * norm0, norm0)
    arrived("z3", zfull.at[pl.ds(0, EX - 1)])
    back = jnp.concatenate(
        [jnp.concatenate([zfull[4 * h + j] for j in range(4)], axis=1) for h in range(2)], axis=0
    )
    image = back * scale + DAMPING * base
    residual = base - fdot(step0, image, TN)

    gram1 = reduced(
        1, residual, fdot(residual, jnp.concatenate([residual, base] * 2, axis=0), NT)
    )
    s0[e] = packed(blocks0)
    push("s0", lambda p: s0.at[e], s0.at[e], e, EX, in_ex)
    norm1 = gram1[:, :Q]
    cross = gram1[:, Q : 2 * Q]
    mixing = fdot(inverse0, norm1)
    blocks1 = rows_of(1)
    s1[e] = packed(blocks1)
    rows1 = jnp.concatenate(blocks1, axis=1) + fdot(mixing, rows0, TN)
    cbuf[e] = fdot(rows1, jnp.concatenate([rows1] * 4, axis=0), NT)
    push("c1", lambda p: cbuf.at[e], cbuf.at[e], e, EX, in_ex)
    push("s1", lambda p: s1.at[e], s1.at[e], e, EX, in_ex)
    gram = (
        norm1
        + fdot(cross, mixing)
        + fdot(mixing, cross, ((0,), (1,)))
        + fdot(mixing, fdot(norm0, mixing), TN)
    )
    to_scalar.wait()
    arrived("s0", s0.at[pl.ds(0, EX - 1)])

    def pick(source, side):
        groups = lax.broadcasted_iota(jnp.int32, (1, R), 1) // Q

        def line(hi, carry):
            for lo in range(Q):
                at = where_s[hi, lo] & (EX * 256 - 1)
                group = where_s[hi, Q + lo]
                row = source[at // 256, pl.ds(at % 256, 1), :]
                picked[side, pl.ds(hi * Q + lo, 1), :] = jnp.where(groups == group, row, 0.0)
            return carry

        lax.fori_loop(0, Q, line, 0)

    pick(s0, 0)
    arrived("c1", cbuf.at[pl.ds(0, EX - 1)])
    total = cbuf[0]
    for s in range(1, EX):
        total = total + cbuf[s]
    step1 = eliminated(total[:, :Q] * (scale * scale) + DAMPING * gram, norm1)
    first = step0 + fdot(mixing, step1)
    sol_ref[...] = fdot(first, base, TN) + fdot(step1, residual, TN)
    arrived("s1", s1.at[pl.ds(0, EX - 1)])
    pick(s1, 1)
    mix = ((0,), (1,))
    scores = fdot(jnp.concatenate([first] * 4, axis=0), picked[0], mix) + fdot(
        jnp.concatenate([step1] * 4, axis=0), picked[1], mix
    )
    score_ref[...] = scores * (1.0 / math.sqrt(K))

    sent("ids", ids_all.at[pl.ds(0, EX - 1)])
    sent("r2", r2.at[pl.ds(0, ZH - 1)])
    sent("r3", right.at[pl.ds(0, GROUP - 1)])
    for c in range(CHUNKS):
        sent(f"l2{c}", l2.at[c, pl.ds(0, ZH - 1)])
    sent("b", bbuf.at[pl.ds(0, 16 * (EX - 1)), :])
    for k in range(2):
        sent(f"y1{k}", y1.at[k, pl.ds(0, GROUP - 1)])
        sent(f"y2{k}", y2.at[k, pl.ds(0, ZH - 1)])
        sent(f"y3{k}", yfull.at[k, pl.ds(0, GROUP - 1)])
    sent("z1", z1.at[pl.ds(0, EX - 1)])
    sent("z3", zfull.at[pl.ds(0, EX - 1)])
    sent("s0", s0.at[pl.ds(0, EX - 1)])
    sent("s1", s1.at[pl.ds(0, EX - 1)])
    sent("c1", cbuf.at[pl.ds(0, EX - 1)])


def local(
    query_states, out_cotangent, query_of_token, gate_weight, up_weight, proj_in, proj_out,
    database, stored_ids,
):
    anywhere = pl.BlockSpec(memory_space=pl.ANY)
    vmem = pl.BlockSpec(memory_space=pltpu.VMEM)
    sol, scores = pl.pallas_call(
        kernel,
        out_shape=(
            jax.ShapeDtypeStruct((Q, COORDS), F32),
            jax.ShapeDtypeStruct((Q, ROWS), F32),
        ),
        in_specs=[anywhere] * 9,
        out_specs=(vmem, vmem),
        scratch_shapes=[
            pltpu.VMEM((TOK, D), BF16),
            pltpu.VMEM((TOK, R), BF16),
            pltpu.VMEM((8, R), jnp.int32),
            pltpu.VMEM((FFL, D), BF16),
            pltpu.VMEM((FFL, D), BF16),
            pltpu.VMEM((FFL, R), BF16),
            pltpu.VMEM((R, R), BF16),
            pltpu.VMEM((ROWS, COORDS), BF16),
            pltpu.VMEM((FFL, CHUNK), F32),
            pltpu.VMEM((FFL, CHUNK), F32),
            pltpu.VMEM((EX, 8, R), jnp.int32),
            pltpu.VMEM((GROUP, R, R), F32),
            pltpu.VMEM((GROUP, R, R), F32),
            pltpu.VMEM((ZH, R, R), F32),
            pltpu.VMEM((GROUP, R, R), F32),
            pltpu.VMEM((CHUNKS, 2, ZH, 4, 8, R), F32),
            pltpu.VMEM((CHUNKS, GROUP, ZH, 8, R), F32),
            pltpu.VMEM((CHUNKS, ZH, 8, R), F32),
            pltpu.VMEM((16 * EX, R), F32),
            pltpu.VMEM((2, GROUP, 2 * Q, R), F32),
            pltpu.VMEM((2, GROUP, 2 * Q, R), F32),
            pltpu.VMEM((2, ZH, 2 * Q, R), F32),
            pltpu.VMEM((2, GROUP, Q, R), F32),
            pltpu.VMEM((EX, 16 + Q, R), F32),
            pltpu.VMEM((EX, 16 + Q, R), F32),
            pltpu.VMEM((EX, 16, R), F32),
            pltpu.VMEM((EX, Q, R), F32),
            pltpu.VMEM((EX, 256, R), F32),
            pltpu.VMEM((EX, 256, R), F32),
            pltpu.VMEM((2, ROWS, R), F32),
            pltpu.VMEM((Q, R), jnp.int32),
            pltpu.SMEM((Q, R), jnp.int32),
            pltpu.SemaphoreType.DMA((7,)),
            pltpu.SemaphoreType.DMA((CHUNKS,)),
            pltpu.SemaphoreType.DMA((2, KSTEPS)),
            pltpu.SemaphoreType.DMA((len(PHASES),)),
            pltpu.SemaphoreType.DMA((len(PHASES),)),
        ],
        compiler_params=pltpu.CompilerParams(
            collective_id=0, has_side_effects=True, vmem_limit_bytes=60 * 1024 * 1024
        ),
        name="logra",
    )(
        query_states,
        out_cotangent,
        query_of_token.reshape(8, R),
        gate_weight.T,
        up_weight.T,
        proj_in,
        proj_out,
        database,
        stored_ids.reshape(8, R),
    )
    return sol.T, scores.T


def solution(mesh):
    both = ("tp", "co")
    in_specs = (
        P("ex", None),
        P("ex", both),
        P("ex"),
        P(None, both),
        P(None, both),
        P(both, None),
        P(both, None),
        P("ex", both),
        P("ex"),
    )
    out_specs = (P(both, None), P("ex", None))
    return jax.shard_map(local, mesh=mesh, in_specs=in_specs, out_specs=out_specs, check_vma=False)
```

time: 294 us -> 127 us (0.43)
  Pallas kernels: 0 us -> 121 us
  blocking collectives: 86.2 us -> 0 us
  waiting for transfers between devices: 76 us -> 0 us
  local copies, waits for them, and re-layouts: 36.1 us -> 3.04 us
  matrix products: 28.7 us -> 0 us
  other arithmetic: 24 us -> 0 us
  starting transfers between devices: 23.8 us -> 0 us
  between operations: 14.6 us -> 0.64 us
    pallas_call x0 -> x1, Pallas kernels: none -> 121 us  [local(): pl.pallas_call(kernel, out_shape=(jax.ShapeDtypeStruct((Q, COORDS), F32),...]
    all_to_all x6 -> x0, blocking collectives: 86.2 us -> none  [the longest x2 36.7 us: sent_and_summed(): lax.all_to_all(split_up(value, dim, devices), axis, 0, 0, tiled=True)]
    all_to_all x5 -> x0, waiting for transfers between devices: 44.2 us -> none  [the longest x4 36.2 us: from_everyone(): lax.all_to_all(jnp.broadcast_to(value[None], (devices, *value.shape)), ax...]
    all_gather x1 -> x0, waiting for transfers between devices: 31.8 us -> none  [in_one_piece(): whole, at, outs = (lax.all_gather(both, axis, axis=dim, tiled=True), 0, [])]
    dot_general x22 -> x0, matrix products: 27.6 us -> none  [the longest x1 9.69 us: local(): jnp.dot(query_states, gate_weight, preferred_element_type=jnp.float32)]
    all_to_all x5 -> x0, starting transfers between devices: 23.5 us -> none  [the longest x4 18.2 us: from_everyone(): lax.all_to_all(jnp.broadcast_to(value[None], (devices, *value.shape)), ax...]
    scatter x1 -> x0, local copies, waits for them, and re-layouts: 21 us -> none  [local(): placed = jnp.zeros((rows_local, all_scores.shape[1]), jnp.float32).at[pos...]
    another operation x15 -> x0, other arithmetic: 20 us -> none  [the longest x9 10.8 us: solve_spd(): factor = jnp.linalg.cholesky(matrix)]
  transfers between devices with their start and end apart: 6 -> 0, of which waited for: 6 -> 0; matrix products, arithmetic and copies ran while one was open for 3% -> 0% of each run, Pallas kernels for 0% -> 0%
where the time goes in v2:
time: 127 us; the launch traced here: 125 us
  Pallas kernels  121 us (95%)
  local copies, waits for them, and re-layouts  3.04 us (2%)
    pallas_call x1, Pallas kernels, local(): pl.pallas_call(kernel, out_shape=(jax.ShapeDtypeStruct((Q, COORDS), F32),...  121 us
    unnamed x2, local copies, waits for them, and re-layouts  3.04 us

profile of v2, /device:TPU:1, one launch (start us, length us, event | category | flops | bytes accessed | tf_op | source)
XLA Modules:
  0.0 125.0 jit_solution(11070782703151029540)
XLA Ops:
  0.6 121.3 %logra.1 = (f32[32,512]{1,0:T(8,128)}, f32[32,1024]{1,0:T(8,128)}) custom-call(bf16[1024,4096]{1,0:T(8,128)(2,1)} %q_hbm.1, bf16[1024,128]{1,0:T(8,128)(2,1)} %cot_hbm.1, s32[8,128]{1,0:T(8,128)} %bitcast.10, bf16[448,4096]{1,0:T(8,128)(2,1)} %bitcast.6, bf16[448,4096]{1,0:T(8,128)(2,1)} %bitcast.7, bf16[448,128]{1,0:T(8,128)(2,1)} %pin_hbm.1, ...), custom_call_target="tpu_custom_call" | custom-call | tf_op jit(solution)/shard_map/logra/pallas_call | solution.py:413
  121.9 1.5 %copy.13 = f32[512,32]{0,1:T(8,128)} copy(f32[512,32]{0,1:T(8,128)} %bitcast.9) | data formatting | bytes 131072
  123.4 1.6 %copy.14 = f32[1024,32]{0,1:T(8,128)} copy(f32[1024,32]{0,1:T(8,128)} %bitcast.8) | data formatting | bytes 262144

commit v3 on v2

v3 whole, which is shorter than its diff:
```python
import functools
import math

import jax
import jax.numpy as jnp
from jax import lax
from jax.experimental import pallas as pl
from jax.experimental.pallas import tpu as pltpu
from jax.sharding import PartitionSpec as P

D = 4096
FFL = 448
TOK = 1024
CHUNK = 256
CHUNKS = TOK // CHUNK
R = 128
Q = 32
QPG = 4
COORDS = 512
ROWS = 1024
EX = 8
GROUP = 8
ZH = 4
K = 16384
NSTORE = 8192
DAMPING = 1.0
HIGHEST = lax.Precision.HIGHEST
MESH = pl.DeviceIdType.MESH
F32 = jnp.float32
BF16 = jnp.bfloat16

PHASES = (
    ["ids", "r1", "r2", "r3"]
    + [f"l1{c}" for c in range(CHUNKS)]
    + ["l2", "gz", "b", "z1", "zg", "z3", "c1"]
    + [f"{name}{k}" for name in ("y1", "y2", "y3", "g1", "g2", "sa", "sb", "fa", "fb") for k in (0, 1)]
)
PHASE = {name: at for at, name in enumerate(PHASES)}


def fdot(a, b, dims=((1,), (0,))):
    return lax.dot_general(a, b, (dims, ((), ())), precision=HIGHEST, preferred_element_type=F32)


def bdot(a, b, dims=((1,), (0,))):
    return lax.dot_general(a, b, (dims, ((), ())), preferred_element_type=F32)


TN = ((0,), (0,))
NT = ((1,), (1,))


def eliminated(matrix, target):
    n = matrix.shape[0]
    both = jnp.concatenate([matrix, target], axis=1)
    lines = lax.broadcasted_iota(jnp.int32, both.shape, 0)
    for k in range(n):
        row = both[k : k + 1, :] / both[k : k + 1, k : k + 1]
        both = jnp.where(lines == k, row, both - both[:, k : k + 1] * row)
    return both[:, n:]


def three_pass(a, b, dims):
    a_high, b_high = a.astype(BF16), b.astype(BF16)
    a_low, b_low = (a - a_high.astype(F32)).astype(BF16), (b - b_high.astype(F32)).astype(BF16)
    return bdot(a_high, b_high, dims) + bdot(a_low, b_high, dims) + bdot(a_high, b_low, dims)


def repeated_gram(a, b):
    return fdot(a, jnp.concatenate([b] * 4, axis=0), NT)


def folded(gram):
    groups = lax.broadcasted_iota(jnp.int32, (8, R), 1) // Q
    out = jnp.where(groups == 0, gram[:8], 0.0)
    for k in range(1, 4):
        out = jnp.where(groups == k, gram[8 * k : 8 * k + 8], out)
    return out


def unfolded(tile):
    parts = [tile] + [pltpu.roll(tile, R - Q * k, 1) for k in range(1, 4)]
    return jnp.concatenate(parts, axis=0)[:, :Q]


def summed(slots):
    total = slots[0]
    for s in slots[1:]:
        total = total + s
    return total


def kernel(
    q_hbm, cot_hbm, qot_hbm, gw_hbm, uw_hbm, pin_hbm, pout_hbm, db_hbm, ids_hbm,
    sol_ref, score_ref,
    q_v, cot_v, qot_v, gw_v, uw_v, pin_v, pout_v, db_v,
    ids_all, rsend, r1, r2s, r2, right,
    lsend, l1, l2s, l2, gsend, gz,
    bbuf,
    ysend, y1, y2, yfull, gram1_v, gram2_v,
    zsend, z1, zg, zfull,
    cbuf, s0, s1, picked, mask_v, where_v, where_s,
    small_sem, q_sem, w_sem, send_sem, recv_sem,
):
    tp = lax.axis_index("tp")
    e = lax.axis_index("ex")
    x = lax.axis_index("co")
    zh = tp // 2
    core = tp % 2
    g = core * 4 + x
    scale = 1.0 / math.sqrt(float(NSTORE))

    def in_group(p):
        return {"tp": zh * 2 + p // 4, "co": p % 4}

    def in_z(p):
        return {"tp": p * 2 + core}

    def in_ex(p):
        return {"ex": p}

    pending = {}

    def send(phase, src, dst, device):
        at = PHASE[phase]
        pltpu.make_async_remote_copy(
            src, dst, send_sem.at[at], recv_sem.at[at], device, MESH
        ).start()

    def push(phase, src_of, dst, me, n, device_of, slots):
        pending[phase] = slots
        for d in range(1, n):
            p = (me + d) % n
            send(phase, src_of(p), dst, device_of(p))

    def arrived(phase):
        slots = pending[phase]
        pltpu.make_async_copy(slots, slots, recv_sem.at[PHASE[phase]]).wait()

    def sent(phase):
        slots = pending.pop(phase)
        pltpu.make_async_copy(slots, slots, send_sem.at[PHASE[phase]]).wait()

    copies = [
        pltpu.make_async_copy(cot_hbm, cot_v, small_sem.at[0]),
        pltpu.make_async_copy(pout_hbm, pout_v, small_sem.at[1]),
        pltpu.make_async_copy(ids_hbm, ids_all.at[e], small_sem.at[2]),
        pltpu.make_async_copy(qot_hbm, qot_v, small_sem.at[3]),
        pltpu.make_async_copy(pin_hbm, pin_v, small_sem.at[4]),
        pltpu.make_async_copy(db_hbm, db_v, small_sem.at[5]),
        pltpu.make_async_copy(gw_hbm, gw_v, w_sem.at[0]),
        pltpu.make_async_copy(uw_hbm, uw_v, w_sem.at[1]),
    ]

    def q_copy(c):
        rows = pl.ds(c * CHUNK, CHUNK)
        return pltpu.make_async_copy(q_hbm.at[rows, :], q_v.at[rows, :], q_sem.at[c])

    for at in (0, 1, 2, 4):
        copies[at].start()
    q_copy(0).start()
    copies[6].start()
    copies[7].start()
    for c in range(1, CHUNKS):
        q_copy(c).start()
    copies[3].start()
    copies[5].start()

    barrier = pltpu.get_barrier_semaphore()
    for n, me, device_of in ((GROUP, g, in_group), (ZH, zh, in_z), (EX, e, in_ex)):
        for d in range(1, n):
            pl.semaphore_signal(
                barrier, inc=1, device_id=device_of((me + d) % n), device_id_type=MESH
            )

    copies[0].wait()
    copies[1].wait()
    rsend[...] = bdot(cot_v[...], pout_v[...]).reshape(ZH, GROUP, Q, R)
    copies[4].wait()
    old = lax.broadcasted_iota(jnp.int32, (R, R), 0)
    new = lax.broadcasted_iota(jnp.int32, (R, R), 1)
    moved = old == 32 * ((new >> 2) & 3) + 4 * (new >> 4) + (new & 3)
    proj = bdot(pin_v[...], jnp.where(moved, 1.0, 0.0).astype(BF16))
    pin_v[...] = proj.astype(BF16)
    copies[2].wait()

    pl.semaphore_wait(barrier, (GROUP - 1) + (ZH - 1) + (EX - 1))
    push(
        "r1", lambda p: rsend.at[:, p], r1.at[g], g, GROUP, in_group, r1.at[pl.ds(0, GROUP - 1)]
    )
    push(
        "ids", lambda p: ids_all.at[e], ids_all.at[e], e, EX, in_ex, ids_all.at[pl.ds(0, EX - 1)]
    )
    r1[g] = rsend[:, g]
    copies[6].wait()
    copies[7].wait()

    def matmul(c):
        q_copy(c).wait()
        a = q_v[c * CHUNK : (c + 1) * CHUNK, :]
        gate = bdot(gw_v[...], a, NT)
        up = bdot(uw_v[...], a, NT)
        hidden = ((gate / (1.0 + jnp.exp(-gate))) * up).astype(BF16)
        lsend[c] = bdot(pin_v[...], hidden, TN).reshape(GROUP, 16, CHUNK)
        push(
            f"l1{c}", lambda p: lsend.at[c, p], l1.at[c, g], g, GROUP, in_group,
            l1.at[c, pl.ds(0, GROUP - 1)],
        )
        l1[c, g] = lsend[c, g]

    pending["l2"] = l2.at[pl.ds(0, ZH - 1)]

    def left_second(c):
        arrived(f"l1{c}")
        l2s[c] = summed([l1[c, s] for s in range(GROUP)])

        @pl.when(zh != c)
        def _():
            send("l2", l2s.at[c], l2.at[zh], in_z(c))

        @pl.when(zh == c)
        def _():
            l2[zh] = l2s[c]

    matmul(0)
    matmul(1)
    left_second(0)
    matmul(2)
    left_second(1)
    matmul(3)

    arrived("r1")
    r2s[...] = summed([r1[s] for s in range(GROUP)])
    push("r2", lambda p: r2s.at[p], r2.at[zh], zh, ZH, in_z, r2.at[pl.ds(0, ZH - 1)])
    r2[zh] = r2s[zh]
    left_second(2)

    arrived("ids")
    kinds = lax.broadcasted_iota(jnp.int32, (Q, R), 0)
    lane = lax.broadcasted_iota(jnp.int32, (Q, R), 1)
    places = jnp.zeros((Q, 2 * Q), F32)
    places_t = jnp.zeros((Q, Q), F32)
    for d in range(EX):
        his, los = [], []
        for r in range(8):
            own = ids_all[(e + d) % EX, pl.ds(r, 1), :] - e * ROWS
            hit_low = (own & 31) == kinds
            part = d + 8 * (r % 2) + 16 * (r // 2)
            his.append(jnp.where((own >> 5) == kinds, 1.0, 0.0).astype(BF16))
            los.append(
                jnp.concatenate(
                    [
                        jnp.where(hit_low, float(part), 0.0),
                        jnp.where(hit_low, lane.astype(F32), 0.0),
                    ],
                    axis=0,
                ).astype(BF16)
            )
        his = jnp.concatenate(his, axis=1)
        los = jnp.concatenate(los, axis=1)
        places = places + bdot(his, los, NT)
        places_t = places_t + bdot(los[:Q], his, NT)
    at = (places[:, :Q].astype(jnp.int32) & 15) * R + places[:, Q:].astype(jnp.int32)
    where_v[...] = jnp.concatenate([at] * 4, axis=1)
    to_scalar = pltpu.make_async_copy(where_v, where_s, small_sem.at[6])
    to_scalar.start()
    group_t = places_t.astype(jnp.int32) >> 4
    for hi in range(Q):
        mask_v[hi * Q : (hi + 1) * Q, :] = jnp.where(
            group_t[:, hi : hi + 1] == (lane >> 5), 1.0, 0.0
        )

    arrived("r2")
    right[g] = summed([r2[s] for s in range(ZH)])
    push(
        "r3", lambda p: right.at[g], right.at[g], g, GROUP, in_group,
        right.at[pl.ds(0, GROUP - 1)],
    )
    left_second(3)
    copies[3].wait()
    query = (
        jnp.concatenate([qot_v[pl.ds(2 * zh, 1), :], qot_v[pl.ds(2 * zh + 1, 1), :]], axis=1)
        - e * QPG
    )
    arrived("r3")
    arrived("l2")
    left = summed([l2[s] for s in range(ZH)])
    weighted = jnp.concatenate([jnp.where(query == k, left, 0.0) for k in range(QPG)], axis=0)
    grads = fdot(weighted, right[...].reshape(CHUNK, R))
    low = lax.broadcasted_iota(jnp.int32, (8, R), 0) < 4
    for p in range(ZH):
        for pair in range(2):
            one, two = [
                grads[q * 16 + 8 * (p // 2) : q * 16 + 8 * (p // 2) + 8]
                for q in (2 * pair, 2 * pair + 1)
            ]
            if p % 2:
                tile = jnp.where(low, pltpu.roll(one, 4, 0), two)
            else:
                tile = jnp.where(low, one, pltpu.roll(two, 4, 0))
            gsend[p, 8 * pair : 8 * pair + 8] = tile
    push("gz", lambda p: gsend.at[p], gz.at[zh], zh, ZH, in_z, gz.at[pl.ds(0, ZH - 1)])
    gz[zh] = gsend[zh]
    arrived("gz")
    own_rows = pl.ds(pl.multiple_of(e * 16, 16), 16)
    bbuf[own_rows, :] = summed([gz[s] for s in range(ZH)])
    push(
        "b", lambda p: bbuf.at[own_rows, :], bbuf.at[own_rows, :], e, EX, in_ex,
        bbuf.at[pl.ds(0, 16 * (EX - 1)), :],
    )
    copies[5].wait()
    arrived("b")
    base = jnp.concatenate([bbuf[pl.ds(i, Q, stride=4), :] for i in range(4)], axis=1)

    def first_stage(k, vectors):
        part = bdot(vectors.astype(BF16), db_v[...], NT)
        for p in range(GROUP):
            ysend[k, p] = part[:, p * R : (p + 1) * R]
        push(
            f"y1{k}", lambda p: ysend.at[k, p], y1.at[k, g], g, GROUP, in_group,
            y1.at[k, pl.ds(0, GROUP - 1)],
        )
        y1[k, g] = ysend[k, g]

    def first_grams(k, tiles):
        rows = pl.ds(0, 8 * len(tiles))
        gram1_v[k, g, rows] = jnp.concatenate(tiles, axis=0)
        push(
            f"g1{k}", lambda p: gram1_v.at[k, g, rows], gram1_v.at[k, g, rows], g, GROUP, in_group,
            gram1_v.at[k, pl.ds(0, GROUP - 1), rows],
        )

    def second_stage(k):
        arrived(f"y1{k}")
        y2[k, zh] = summed([y1[k, s] for s in range(GROUP)])
        push(
            f"y2{k}", lambda p: y2.at[k, zh], y2.at[k, zh], zh, ZH, in_z,
            y2.at[k, pl.ds(0, ZH - 1)],
        )

    def second_grams(k, count):
        rows = pl.ds(0, 8 * count)
        arrived(f"g1{k}")
        gram2_v[k, zh, rows] = summed([gram1_v[k, s, rows] for s in range(GROUP)])
        push(
            f"g2{k}", lambda p: gram2_v.at[k, zh, rows], gram2_v.at[k, zh, rows], zh, ZH, in_z,
            gram2_v.at[k, pl.ds(0, ZH - 1), rows],
        )

    def third_stage(k):
        arrived(f"y2{k}")
        yfull[k, g] = summed([y2[k, s] for s in range(ZH)])
        push(
            f"y3{k}", lambda p: yfull.at[k, g], yfull.at[k, g], g, GROUP, in_group,
            yfull.at[k, pl.ds(0, GROUP - 1)],
        )

    def grams_of(k, count):
        rows = pl.ds(0, 8 * count)
        arrived(f"g2{k}")
        total = summed([gram2_v[k, s, rows] for s in range(ZH)])
        return [unfolded(total[8 * at : 8 * at + 8]) for at in range(count)]

    def rows_of(k):
        arrived(f"y3{k}")
        return [yfull[k, s] for s in range(GROUP)]

    def own_packed(buf, blocks):
        for h in range(2):
            tall = jnp.concatenate([blocks[2 * i + h] for i in range(4)], axis=0)
            buf[h * ROWS : h * ROWS + R, :] = tall.T

    def half(d, count=1):
        return pl.ds(pl.multiple_of(core * ROWS + d * R, R), count * R)

    def spread(k, buf):
        for name, lo, hi in (("sa", 4, 8), ("sb", 1, 4)):
            pending[f"{name}{k}"] = buf.at[half(lo, hi - lo), :]
            for slot in range(lo, hi):
                send(f"{name}{k}", buf.at[half(0), :], buf.at[half(slot), :], in_ex((e - slot) % EX))

    def forward(k, buf, name):
        lo, hi = (4, 8) if name == "a" else (1, 4)
        arrived(f"s{name}{k}")
        part = buf.at[half(lo, hi - lo), :]
        pending[f"f{name}{k}"] = part
        send(f"f{name}{k}", part, part, {"tp": zh * 2 + (1 - core)})

    first_stage(0, base)
    first_grams(0, [folded(repeated_gram(base, base))])
    second_stage(0)
    second_grams(0, 1)
    third_stage(0)
    (norm0,) = grams_of(0, 1)
    eye = (
        lax.broadcasted_iota(jnp.int32, (Q, Q), 0) == lax.broadcasted_iota(jnp.int32, (Q, Q), 1)
    ).astype(F32)
    inverse0 = eliminated(norm0, eye)
    blocks0 = rows_of(0)
    rows0 = jnp.concatenate(blocks0, axis=1)

    back = bdot((rows0 * scale).astype(BF16), db_v[...])
    for p in range(EX):
        zsend[p] = back[16 * (p // 4) : 16 * (p // 4) + 16, (p % 4) * R : (p % 4 + 1) * R]
    push("z1", lambda p: zsend.at[p], z1.at[e], e, EX, in_ex, z1.at[pl.ds(0, EX - 1)])
    z1[e] = zsend[e]
    zg[e] = folded(repeated_gram(rows0, rows0))
    push("zg", lambda p: zg.at[e], zg.at[e], e, EX, in_ex, zg.at[pl.ds(0, EX - 1)])
    own_packed(s0, blocks0)
    arrived("z1")
    zfull[e] = summed([z1[s] for s in range(EX)])
    push("z3", lambda p: zfull.at[e], zfull.at[e], e, EX, in_ex, zfull.at[pl.ds(0, EX - 1)])
    arrived("zg")
    row_gram = unfolded(summed([zg[s] for s in range(EX)]))
    step0 = eliminated(row_gram * (scale * scale) + DAMPING * norm0, norm0)
    arrived("z3")
    spread(0, s0)
    back = jnp.concatenate(
        [jnp.concatenate([zfull[4 * h + j] for j in range(4)], axis=1) for h in range(2)], axis=0
    )
    image = back * scale + DAMPING * base
    residual = base - fdot(step0, image, TN)

    first_stage(1, residual)
    first_grams(
        1, [folded(repeated_gram(residual, residual)), folded(repeated_gram(residual, base))]
    )
    second_stage(1)
    second_grams(1, 2)
    forward(0, s0, "a")
    forward(0, s0, "b")
    to_scalar.wait()
    third_stage(1)
    norm1, cross = grams_of(1, 2)
    mixing = fdot(inverse0, norm1)

    def pick(source, side):
        def line(hi, carry):
            for lo in range(Q):
                at = where_s[hi, lo] & (2 * ROWS - 1)
                picked[side, pl.ds(hi * Q + lo, 1), :] = source[pl.ds(at, 1), :]
            return carry

        lax.fori_loop(0, Q, line, 0)

    arrived("fa0")
    arrived("fb0")
    pick(s0, 0)
    blocks1 = rows_of(1)
    rows1 = jnp.concatenate(blocks1, axis=1) + fdot(mixing, rows0, TN)
    cbuf[e] = folded(repeated_gram(rows1, rows1))
    push("c1", lambda p: cbuf.at[e], cbuf.at[e], e, EX, in_ex, cbuf.at[pl.ds(0, EX - 1)])
    own_packed(s1, blocks1)
    spread(1, s1)
    gram = (
        norm1
        + fdot(cross, mixing)
        + fdot(mixing, cross, ((0,), (1,)))
        + fdot(mixing, fdot(norm0, mixing), TN)
    )
    arrived("c1")
    row_gram = unfolded(summed([cbuf[s] for s in range(EX)]))
    step1 = eliminated(row_gram * (scale * scale) + DAMPING * gram, norm1)
    forward(1, s1, "a")
    first = step0 + fdot(mixing, step1)
    sol_ref[...] = fdot(first, base, TN) + fdot(step1, residual, TN)
    forward(1, s1, "b")
    arrived("fa1")
    arrived("fb1")
    pick(s1, 1)
    mask = mask_v[...]
    chosen = jnp.concatenate([picked[0] * mask, picked[1] * mask], axis=1)
    coeffs = jnp.concatenate([first] * 4 + [step1] * 4, axis=0) * (1.0 / math.sqrt(K))
    score_ref[...] = three_pass(coeffs, chosen, ((0,), (1,)))

    for phase in list(pending):
        sent(phase)


def local(
    query_states, out_cotangent, query_of_token, gate_weight, up_weight, proj_in, proj_out,
    database, stored_ids,
):
    anywhere = pl.BlockSpec(memory_space=pl.ANY)
    vmem = pl.BlockSpec(memory_space=pltpu.VMEM)
    sol, scores = pl.pallas_call(
        kernel,
        out_shape=(
            jax.ShapeDtypeStruct((Q, COORDS), F32),
            jax.ShapeDtypeStruct((Q, ROWS), F32),
        ),
        in_specs=[anywhere] * 9,
        out_specs=(vmem, vmem),
        scratch_shapes=[
            pltpu.VMEM((TOK, D), BF16),
            pltpu.VMEM((TOK, R), BF16),
            pltpu.VMEM((8, R), jnp.int32),
            pltpu.VMEM((FFL, D), BF16),
            pltpu.VMEM((FFL, D), BF16),
            pltpu.VMEM((FFL, R), BF16),
            pltpu.VMEM((R, R), BF16),
            pltpu.VMEM((ROWS, COORDS), BF16),
            pltpu.VMEM((EX, 8, R), jnp.int32),
            pltpu.VMEM((ZH, GROUP, Q, R), F32),
            pltpu.VMEM((GROUP, ZH, Q, R), F32),
            pltpu.VMEM((ZH, Q, R), F32),
            pltpu.VMEM((ZH, Q, R), F32),
            pltpu.VMEM((GROUP, Q, R), F32),
            pltpu.VMEM((CHUNKS, GROUP, 16, CHUNK), F32),
            pltpu.VMEM((CHUNKS, GROUP, 16, CHUNK), F32),
            pltpu.VMEM((CHUNKS, 16, CHUNK), F32),
            pltpu.VMEM((ZH, 16, CHUNK), F32),
            pltpu.VMEM((ZH, 16, R), F32),
            pltpu.VMEM((ZH, 16, R), F32),
            pltpu.VMEM((16 * EX, R), F32),
            pltpu.VMEM((2, GROUP, Q, R), F32),
            pltpu.VMEM((2, GROUP, Q, R), F32),
            pltpu.VMEM((2, ZH, Q, R), F32),
            pltpu.VMEM((2, GROUP, Q, R), F32),
            pltpu.VMEM((2, GROUP, 16, R), F32),
            pltpu.VMEM((2, ZH, 16, R), F32),
            pltpu.VMEM((EX, 16, R), F32),
            pltpu.VMEM((EX, 16, R), F32),
            pltpu.VMEM((EX, 8, R), F32),
            pltpu.VMEM((EX, 16, R), F32),
            pltpu.VMEM((EX, 8, R), F32),
            pltpu.VMEM((2 * ROWS, R), F32),
            pltpu.VMEM((2 * ROWS, R), F32),
            pltpu.VMEM((2, ROWS, R), F32),
            pltpu.VMEM((ROWS, R), F32),
            pltpu.VMEM((Q, R), jnp.int32),
            pltpu.SMEM((Q, R), jnp.int32),
            pltpu.SemaphoreType.DMA((7,)),
            pltpu.SemaphoreType.DMA((CHUNKS,)),
            pltpu.SemaphoreType.DMA((2,)),
            pltpu.SemaphoreType.DMA((len(PHASES),)),
            pltpu.SemaphoreType.DMA((len(PHASES),)),
        ],
        compiler_params=pltpu.CompilerParams(
            collective_id=0, has_side_effects=True, vmem_limit_bytes=60 * 1024 * 1024
        ),
        name="logra",
    )(
        query_states,
        out_cotangent,
        query_of_token.reshape(8, R),
        gate_weight.T,
        up_weight.T,
        proj_in,
        proj_out,
        database,
        stored_ids.reshape(8, R),
    )
    return sol.T, scores.T


def solution(mesh):
    both = ("tp", "co")
    in_specs = (
        P("ex", None),
        P("ex", both),
        P("ex"),
        P(None, both),
        P(None, both),
        P(both, None),
        P(both, None),
        P("ex", both),
        P("ex"),
    )
    out_specs = (P(both, None), P("ex", None))
    return jax.shard_map(local, mesh=mesh, in_specs=in_specs, out_specs=out_specs, check_vma=False)
```

time: 127 us -> 99.3 us (0.78); the launches traced: 125 us -> 99.1 us
  Pallas kernels: 121 us -> 95.5 us
    pallas_call x1, Pallas kernels: 121 us -> 95.5 us  [local(): pl.pallas_call(kernel, out_shape=(jax.ShapeDtypeStruct((Q, COORDS), F32),...]
where the time goes in v3:
time: 99.3 us; the launch traced here: 99.1 us
  Pallas kernels  95.5 us (96%)
  local copies, waits for them, and re-layouts  3.04 us (3%)
    pallas_call x1, Pallas kernels, local(): pl.pallas_call(kernel, out_shape=(jax.ShapeDtypeStruct((Q, COORDS), F32),...  95.5 us
    unnamed x2, local copies, waits for them, and re-layouts  3.04 us

profile of v3, /device:TPU:1, one launch (start us, length us, event | category | flops | bytes accessed | tf_op | source)
XLA Modules:
  0.0 99.1 jit_solution(325191832265941571)
XLA Ops:
  0.6 95.5 %logra.1 = (f32[32,512]{1,0:T(8,128)}, f32[32,1024]{1,0:T(8,128)}) custom-call(bf16[1024,4096]{1,0:T(8,128)(2,1)} %q_hbm.1, bf16[1024,128]{1,0:T(8,128)(2,1)} %cot_hbm.1, s32[8,128]{1,0:T(8,128)} %bitcast.10, bf16[448,4096]{1,0:T(8,128)(2,1)} %bitcast.6, bf16[448,4096]{1,0:T(8,128)(2,1)} %bitcast.7, bf16[448,128]{1,0:T(8,128)(2,1)} %pin_hbm.1, ...), custom_call_target="tpu_custom_call" | custom-call | tf_op jit(solution)/shard_map/logra/pallas_call | solution.py:486
  96.1 1.5 %copy.13 = f32[512,32]{0,1:T(8,128)} copy(f32[512,32]{0,1:T(8,128)} %bitcast.9) | data formatting | bytes 131072
  97.6 1.6 %copy.14 = f32[1024,32]{0,1:T(8,128)} copy(f32[1024,32]{0,1:T(8,128)} %bitcast.8) | data formatting | bytes 262144

commit v4 on v3

--- a/solution.py
+++ b/solution.py
@@ -32,9 +32,10 @@
 PHASES = (
     ["ids", "r1", "r2", "r3"]
     + [f"l1{c}" for c in range(CHUNKS)]
-    + ["l2", "gz", "b", "z1", "zg", "z3", "c1"]
+    + ["l2", "gz", "b", "z1", "zg", "z3", "c1", "c2"]
     + [f"{name}{k}" for name in ("y1", "y2", "y3", "g1", "g2", "sa", "sb", "fa", "fb") for k in (0, 1)]
 )
+FAR_FIRST = {4: (2, 1), 5: (1, 1), 6: (3, 1), 7: (2, 0), 1: (1, 0), 2: (3, 0), 3: (0, 1)}
 PHASE = {name: at for at, name in enumerate(PHASES)}
 
 
@@ -92,14 +93,14 @@
 
 def kernel(
     q_hbm, cot_hbm, qot_hbm, gw_hbm, uw_hbm, pin_hbm, pout_hbm, db_hbm, ids_hbm,
-    sol_ref, score_ref,
+    out_ref,
     q_v, cot_v, qot_v, gw_v, uw_v, pin_v, pout_v, db_v,
     ids_all, rsend, r1, r2s, r2, right,
     lsend, l1, l2s, l2, gsend, gz,
     bbuf,
     ysend, y1, y2, yfull, gram1_v, gram2_v,
     zsend, z1, zg, zfull,
-    cbuf, s0, s1, picked, mask_v, where_v, where_s,
+    cbuf, dbuf, s0, s1, picked, mask_v, where_v, where_s,
     small_sem, q_sem, w_sem, send_sem, recv_sem,
 ):
     tp = lax.axis_index("tp")
@@ -119,6 +120,21 @@
     def in_ex(p):
         return {"ex": p}
 
+    y, z_lo = e // 2, e % 2
+
+    def peers(me, n):
+        if n == ZH:
+            return [(zh + d) % ZH for d in (2, 1, 3)]
+        if me is e:
+            return [
+                ((y + dy) % 4) * 2 + (z_lo + dz) % 2
+                for dy, dz in ((2, 1), (2, 0), (1, 1), (3, 1), (1, 0), (3, 0), (0, 1))
+            ]
+        return [
+            ((core + dc) % 2) * 4 + (x + dx) % 4
+            for dx, dc in ((2, 1), (2, 0), (1, 1), (3, 1), (1, 0), (3, 0), (0, 1))
+        ]
+
     pending = {}
 
     def send(phase, src, dst, device):
@@ -129,8 +145,7 @@
 
     def push(phase, src_of, dst, me, n, device_of, slots):
         pending[phase] = slots
-        for d in range(1, n):
-            p = (me + d) % n
+        for p in peers(me, n):
             send(phase, src_of(p), dst, device_of(p))
 
     def arrived(phase):
@@ -156,6 +171,11 @@
         rows = pl.ds(c * CHUNK, CHUNK)
         return pltpu.make_async_copy(q_hbm.at[rows, :], q_v.at[rows, :], q_sem.at[c])
 
+    barrier = pltpu.get_barrier_semaphore()
+    for n, me, device_of in ((ZH, zh, in_z), (EX, e, in_ex), (GROUP, g, in_group)):
+        for p in peers(me, n):
+            pl.semaphore_signal(barrier, inc=1, device_id=device_of(p), device_id_type=MESH)
+
     for at in (0, 1, 2, 4):
         copies[at].start()
     q_copy(0).start()
@@ -166,32 +186,25 @@
     copies[3].start()
     copies[5].start()
 
-    barrier = pltpu.get_barrier_semaphore()
-    for n, me, device_of in ((GROUP, g, in_group), (ZH, zh, in_z), (EX, e, in_ex)):
-        for d in range(1, n):
-            pl.semaphore_signal(
-                barrier, inc=1, device_id=device_of((me + d) % n), device_id_type=MESH
-            )
-
     copies[0].wait()
     copies[1].wait()
     rsend[...] = bdot(cot_v[...], pout_v[...]).reshape(ZH, GROUP, Q, R)
+    copies[2].wait()
+
+    pl.semaphore_wait(barrier, (GROUP - 1) + (ZH - 1) + (EX - 1))
+    push(
+        "r1", lambda p: rsend.at[:, p], r1.at[g], g, GROUP, in_group, r1.at[pl.ds(0, GROUP - 1)]
+    )
+    push(
+        "ids", lambda p: ids_all.at[e], ids_all.at[e], e, EX, in_ex, ids_all.at[pl.ds(0, EX - 1)]
+    )
+    r1[g] = rsend[:, g]
     copies[4].wait()
     old = lax.broadcasted_iota(jnp.int32, (R, R), 0)
     new = lax.broadcasted_iota(jnp.int32, (R, R), 1)
     moved = old == 32 * ((new >> 2) & 3) + 4 * (new >> 4) + (new & 3)
     proj = bdot(pin_v[...], jnp.where(moved, 1.0, 0.0).astype(BF16))
     pin_v[...] = proj.astype(BF16)
-    copies[2].wait()
-
-    pl.semaphore_wait(barrier, (GROUP - 1) + (ZH - 1) + (EX - 1))
-    push(
-        "r1", lambda p: rsend.at[:, p], r1.at[g], g, GROUP, in_group, r1.at[pl.ds(0, GROUP - 1)]
-    )
-    push(
-        "ids", lambda p: ids_all.at[e], ids_all.at[e], e, EX, in_ex, ids_all.at[pl.ds(0, EX - 1)]
-    )
-    r1[g] = rsend[:, g]
     copies[6].wait()
     copies[7].wait()
 
@@ -208,9 +221,8 @@
         )
         l1[c, g] = lsend[c, g]
 
-    pending["l2"] = l2.at[pl.ds(0, ZH - 1)]
-
     def left_second(c):
+        pending["l2"] = l2.at[pl.ds(0, ZH - 1)]
         arrived(f"l1{c}")
         l2s[c] = summed([l1[c, s] for s in range(GROUP)])
 
@@ -224,15 +236,14 @@
 
     matmul(0)
     matmul(1)
-    left_second(0)
     matmul(2)
-    left_second(1)
-    matmul(3)
-
     arrived("r1")
     r2s[...] = summed([r1[s] for s in range(GROUP)])
     push("r2", lambda p: r2s.at[p], r2.at[zh], zh, ZH, in_z, r2.at[pl.ds(0, ZH - 1)])
     r2[zh] = r2s[zh]
+    matmul(3)
+    left_second(0)
+    left_second(1)
     left_second(2)
 
     arrived("ids")
@@ -241,9 +252,11 @@
     places = jnp.zeros((Q, 2 * Q), F32)
     places_t = jnp.zeros((Q, Q), F32)
     for d in range(EX):
+        dy, dz = FAR_FIRST[d] if d else (0, 0)
+        source = ((y + dy) % 4) * 2 + (z_lo + dz) % 2
         his, los = [], []
         for r in range(8):
-            own = ids_all[(e + d) % EX, pl.ds(r, 1), :] - e * ROWS
+            own = ids_all[source, pl.ds(r, 1), :] - e * ROWS
             hit_low = (own & 31) == kinds
             part = d + 8 * (r % 2) + 16 * (r // 2)
             his.append(jnp.where((own >> 5) == kinds, 1.0, 0.0).astype(BF16))
@@ -377,7 +390,9 @@
         for name, lo, hi in (("sa", 4, 8), ("sb", 1, 4)):
             pending[f"{name}{k}"] = buf.at[half(lo, hi - lo), :]
             for slot in range(lo, hi):
-                send(f"{name}{k}", buf.at[half(0), :], buf.at[half(slot), :], in_ex((e - slot) % EX))
+                dy, dz = FAR_FIRST[slot]
+                p = ((y - dy) % 4) * 2 + (z_lo + dz) % 2
+                send(f"{name}{k}", buf.at[half(0), :], buf.at[half(slot), :], in_ex(p))
 
     def forward(k, buf, name):
         lo, hi = (4, 8) if name == "a" else (1, 4)
@@ -431,6 +446,11 @@
     forward(0, s0, "b")
     to_scalar.wait()
     third_stage(1)
+    block0, block1 = yfull[0, g], yfull[1, g]
+    cbuf[e] = jnp.concatenate(
+        [folded(repeated_gram(block1, block1)), folded(repeated_gram(block1, block0))], axis=0
+    )
+    push("c1", lambda p: cbuf.at[e], cbuf.at[e], e, EX, in_ex, cbuf.at[pl.ds(0, EX - 1)])
     norm1, cross = grams_of(1, 2)
     mixing = fdot(inverse0, norm1)
 
@@ -443,14 +463,11 @@
 
         lax.fori_loop(0, Q, line, 0)
 
-    arrived("fa0")
-    arrived("fb0")
-    pick(s0, 0)
     blocks1 = rows_of(1)
-    rows1 = jnp.concatenate(blocks1, axis=1) + fdot(mixing, rows0, TN)
-    cbuf[e] = folded(repeated_gram(rows1, rows1))
-    push("c1", lambda p: cbuf.at[e], cbuf.at[e], e, EX, in_ex, cbuf.at[pl.ds(0, EX - 1)])
     own_packed(s1, blocks1)
+    arrived("c1")
+    dbuf[g] = summed([cbuf[s] for s in range(EX)])
+    push("c2", lambda p: dbuf.at[g], dbuf.at[g], g, GROUP, in_group, dbuf.at[pl.ds(0, GROUP - 1)])
     spread(1, s1)
     gram = (
         norm1
@@ -458,20 +475,30 @@
         + fdot(mixing, cross, ((0,), (1,)))
         + fdot(mixing, fdot(norm0, mixing), TN)
     )
-    arrived("c1")
-    row_gram = unfolded(summed([cbuf[s] for s in range(EX)]))
-    step1 = eliminated(row_gram * (scale * scale) + DAMPING * gram, norm1)
+    arrived("fa0")
+    arrived("fb0")
+    pick(s0, 0)
+    arrived("c2")
+    total = summed([dbuf[s] for s in range(GROUP)])
+    square, mixed = unfolded(total[:8]), unfolded(total[8:])
+    rows_gram = (
+        square
+        + fdot(mixed, mixing)
+        + fdot(mixing, mixed, ((0,), (1,)))
+        + fdot(mixing, fdot(row_gram, mixing), TN)
+    )
+    step1 = eliminated(rows_gram * (scale * scale) + DAMPING * gram, norm1)
     forward(1, s1, "a")
     first = step0 + fdot(mixing, step1)
-    sol_ref[...] = fdot(first, base, TN) + fdot(step1, residual, TN)
+    out_ref[:, :COORDS] = fdot(first, base, TN) + fdot(step1, residual, TN)
     forward(1, s1, "b")
     arrived("fa1")
     arrived("fb1")
     pick(s1, 1)
     mask = mask_v[...]
     chosen = jnp.concatenate([picked[0] * mask, picked[1] * mask], axis=1)
-    coeffs = jnp.concatenate([first] * 4 + [step1] * 4, axis=0) * (1.0 / math.sqrt(K))
-    score_ref[...] = three_pass(coeffs, chosen, ((0,), (1,)))
+    coeffs = jnp.concatenate([first] * 4 + [step1] * 4, axis=0)
+    out_ref[:, COORDS:] = three_pass(coeffs, chosen, ((0,), (1,)))
 
     for phase in list(pending):
         sent(phase)
@@ -483,14 +510,11 @@
 ):
     anywhere = pl.BlockSpec(memory_space=pl.ANY)
     vmem = pl.BlockSpec(memory_space=pltpu.VMEM)
-    sol, scores = pl.pallas_call(
+    out = pl.pallas_call(
         kernel,
-        out_shape=(
-            jax.ShapeDtypeStruct((Q, COORDS), F32),
-            jax.ShapeDtypeStruct((Q, ROWS), F32),
-        ),
+        out_shape=jax.ShapeDtypeStruct((Q, COORDS + ROWS), F32),
         in_specs=[anywhere] * 9,
-        out_specs=(vmem, vmem),
+        out_specs=vmem,
         scratch_shapes=[
             pltpu.VMEM((TOK, D), BF16),
             pltpu.VMEM((TOK, R), BF16),
@@ -523,7 +547,8 @@
             pltpu.VMEM((EX, 16, R), F32),
             pltpu.VMEM((EX, 8, R), F32),
             pltpu.VMEM((EX, 16, R), F32),
-            pltpu.VMEM((EX, 8, R), F32),
+            pltpu.VMEM((EX, 16, R), F32),
+            pltpu.VMEM((GROUP, 16, R), F32),
             pltpu.VMEM((2 * ROWS, R), F32),
             pltpu.VMEM((2 * ROWS, R), F32),
             pltpu.VMEM((2, ROWS, R), F32),
@@ -551,7 +576,7 @@
         database,
         stored_ids.reshape(8, R),
     )
-    return sol.T, scores.T
+    return out[:, :COORDS].T, out[:, COORDS:].T * (1.0 / math.sqrt(K))
 
 
 def solution(mesh):

time: 99.3 us -> 90.5 us (0.911)
  Pallas kernels: 95.5 us -> 86.7 us
  other arithmetic: 0 us -> 1.57 us
  local copies, waits for them, and re-layouts: 3.04 us -> 1.47 us
    pallas_call x1, Pallas kernels: 95.5 us -> 86.7 us  [local(): pl.pallas_call(kernel, out_shape=jax.ShapeDtypeStruct((Q, COORDS + ROWS),...]
    unnamed x2 -> x0, local copies, waits for them, and re-layouts: 3.04 us -> none
    mul x0 -> x1, other arithmetic: none -> 1.57 us  [local(): return (out[:, :COORDS].T, out[:, COORDS:].T * (1.0 / math.sqrt(K)))]
    transpose x0 -> x1, local copies, waits for them, and re-layouts: none -> 1.47 us  [local(): return (out[:, :COORDS].T, out[:, COORDS:].T * (1.0 / math.sqrt(K)))]
where the time goes in v4:
time: 90.5 us; the launch traced here: 90.3 us
  Pallas kernels  86.7 us (96%)
  other arithmetic  1.57 us (2%)
  local copies, waits for them, and re-layouts  1.47 us (2%)
    pallas_call x1, Pallas kernels, local(): pl.pallas_call(kernel, out_shape=jax.ShapeDtypeStruct((Q, COORDS + ROWS),...  86.7 us

profile of v4, /device:TPU:1, one launch (start us, length us, event | category | flops | bytes accessed | tf_op | source)
XLA Modules:
  0.0 90.3 jit_solution(9758766004952861593)
XLA Ops:
  0.6 86.7 %logra.1 = f32[32,1536]{1,0:T(8,128)} custom-call(bf16[1024,4096]{1,0:T(8,128)(2,1)} %q_hbm.1, bf16[1024,128]{1,0:T(8,128)(2,1)} %cot_hbm.1, s32[8,128]{1,0:T(8,128)} %bitcast.10, bf16[448,4096]{1,0:T(8,128)(2,1)} %bitcast.8, bf16[448,4096]{1,0:T(8,128)(2,1)} %bitcast.9, bf16[448,128]{1,0:T(8,128)(2,1)} %pin_hbm.1, bf16[128,128]{1,0:T(8,128)(2,1)} %pout_hbm.1, ...), custom_call_target="tpu_custom_call" | custom-call | tf_op jit(solution)/shard_map/logra/pallas_call | solution.py:513
  87.3 1.5 %slice_bitcast_fusion = f32[512,32]{0,1:T(8,128)} fusion(f32[32,1536]{1,0:T(8,128)} %logra.1), kind=kLoop, calls=%fused_computation.1 | loop fusion | bytes 131072 | tf_op jit(solution)/shard_map/transpose | solution.py:579
  88.8 1.6 %multiply_bitcast_fusion = f32[1024,32]{0,1:T(8,128)} fusion(f32[32,1536]{1,0:T(8,128)} %logra.1), kind=kLoop, calls=%fused_computation | loop fusion | flops 32768 | bytes 262144 | tf_op jit(solution)/shard_map/mul | solution.py:579

commit v5 on v4

--- a/solution.py
+++ b/solution.py
@@ -32,7 +32,7 @@
 PHASES = (
     ["ids", "r1", "r2", "r3"]
     + [f"l1{c}" for c in range(CHUNKS)]
-    + ["l2", "gz", "b", "z1", "zg", "z3", "c1", "c2"]
+    + ["l2", "gz", "b", "z1", "zg", "z3", "c1", "c2", "ma", "mx"]
     + [f"{name}{k}" for name in ("y1", "y2", "y3", "g1", "g2", "sa", "sb", "fa", "fb") for k in (0, 1)]
 )
 FAR_FIRST = {4: (2, 1), 5: (1, 1), 6: (3, 1), 7: (2, 0), 1: (1, 0), 2: (3, 0), 3: (0, 1)}
@@ -100,7 +100,7 @@
     bbuf,
     ysend, y1, y2, yfull, gram1_v, gram2_v,
     zsend, z1, zg, zfull,
-    cbuf, dbuf, s0, s1, picked, mask_v, where_v, where_s,
+    cbuf, dbuf, far, s0, s1, picked, mask_v, where_v, where_s,
     small_sem, q_sem, w_sem, send_sem, recv_sem,
 ):
     tp = lax.axis_index("tp")
@@ -258,7 +258,7 @@
         for r in range(8):
             own = ids_all[source, pl.ds(r, 1), :] - e * ROWS
             hit_low = (own & 31) == kinds
-            part = d + 8 * (r % 2) + 16 * (r // 2)
+            part = d + 8 * (r // 4) + 16 * (r % 4)
             his.append(jnp.where((own >> 5) == kinds, 1.0, 0.0).astype(BF16))
             los.append(
                 jnp.concatenate(
@@ -380,14 +380,14 @@
 
     def own_packed(buf, blocks):
         for h in range(2):
-            tall = jnp.concatenate([blocks[2 * i + h] for i in range(4)], axis=0)
+            tall = jnp.concatenate(blocks[4 * h : 4 * h + 4], axis=0)
             buf[h * ROWS : h * ROWS + R, :] = tall.T
 
     def half(d, count=1):
         return pl.ds(pl.multiple_of(core * ROWS + d * R, R), count * R)
 
-    def spread(k, buf):
-        for name, lo, hi in (("sa", 4, 8), ("sb", 1, 4)):
+    def spread(k, buf, parts):
+        for name, lo, hi in parts:
             pending[f"{name}{k}"] = buf.at[half(lo, hi - lo), :]
             for slot in range(lo, hi):
                 dy, dz = FAR_FIRST[slot]
@@ -396,7 +396,8 @@
 
     def forward(k, buf, name):
         lo, hi = (4, 8) if name == "a" else (1, 4)
-        arrived(f"s{name}{k}")
+        if f"s{name}{k}" in pending:
+            arrived(f"s{name}{k}")
         part = buf.at[half(lo, hi - lo), :]
         pending[f"f{name}{k}"] = part
         send(f"f{name}{k}", part, part, {"tp": zh * 2 + (1 - core)})
@@ -429,7 +430,7 @@
     row_gram = unfolded(summed([zg[s] for s in range(EX)]))
     step0 = eliminated(row_gram * (scale * scale) + DAMPING * norm0, norm0)
     arrived("z3")
-    spread(0, s0)
+    spread(0, s0, (("sa", 4, 8), ("sb", 1, 4)))
     back = jnp.concatenate(
         [jnp.concatenate([zfull[4 * h + j] for j in range(4)], axis=1) for h in range(2)], axis=0
     )
@@ -446,6 +447,11 @@
     forward(0, s0, "b")
     to_scalar.wait()
     third_stage(1)
+    pending["ma"] = far.at[0]
+    for slot in range(4, 8):
+        dy, dz = FAR_FIRST[slot]
+        p = ((y - dy) % 4) * 2 + (z_lo + dz) % 2
+        send("ma", yfull.at[1, g], far.at[x, slot - 4], in_ex(p))
     block0, block1 = yfull[0, g], yfull[1, g]
     cbuf[e] = jnp.concatenate(
         [folded(repeated_gram(block1, block1)), folded(repeated_gram(block1, block0))], axis=0
@@ -468,7 +474,11 @@
     arrived("c1")
     dbuf[g] = summed([cbuf[s] for s in range(EX)])
     push("c2", lambda p: dbuf.at[g], dbuf.at[g], g, GROUP, in_group, dbuf.at[pl.ds(0, GROUP - 1)])
-    spread(1, s1)
+    spread(1, s1, (("sb", 1, 4),))
+    arrived("ma")
+    pending["mx"] = far.at[pl.ds(0, 3)]
+    for dx in (2, 1, 3):
+        send("mx", far.at[x], far.at[x], {"co": (x + dx) % 4})
     gram = (
         norm1
         + fdot(cross, mixing)
@@ -487,11 +497,15 @@
         + fdot(mixing, mixed, ((0,), (1,)))
         + fdot(mixing, fdot(row_gram, mixing), TN)
     )
+    forward(1, s1, "b")
     step1 = eliminated(rows_gram * (scale * scale) + DAMPING * gram, norm1)
+    arrived("mx")
+    for slot in range(4, 8):
+        tall = jnp.concatenate([far[s, slot - 4] for s in range(4)], axis=0)
+        s1[half(slot), :] = tall.T
     forward(1, s1, "a")
     first = step0 + fdot(mixing, step1)
     out_ref[:, :COORDS] = fdot(first, base, TN) + fdot(step1, residual, TN)
-    forward(1, s1, "b")
     arrived("fa1")
     arrived("fb1")
     pick(s1, 1)
@@ -512,7 +526,7 @@
     vmem = pl.BlockSpec(memory_space=pltpu.VMEM)
     out = pl.pallas_call(
         kernel,
-        out_shape=jax.ShapeDtypeStruct((Q, COORDS + ROWS), F32),
+        out_shape=pltpu.VMEM((Q, COORDS + ROWS), F32),
         in_specs=[anywhere] * 9,
         out_specs=vmem,
         scratch_shapes=[
@@ -549,6 +563,7 @@
             pltpu.VMEM((EX, 16, R), F32),
             pltpu.VMEM((EX, 16, R), F32),
             pltpu.VMEM((GROUP, 16, R), F32),
+            pltpu.VMEM((4, 4, Q, R), F32),
             pltpu.VMEM((2 * ROWS, R), F32),
             pltpu.VMEM((2 * ROWS, R), F32),
             pltpu.VMEM((2, ROWS, R), F32),

time: 90.5 us -> 87.7 us (0.969)
  Pallas kernels: 86.7 us -> 85.6 us
    pallas_call x1, Pallas kernels: 86.7 us -> 85.6 us  [local(): pl.pallas_call(kernel, out_shape=pltpu.VMEM((Q, COORDS + ROWS), F32), in_...]
where the time goes in v5:
time: 87.7 us; the launch traced here: 87.6 us
  Pallas kernels  85.6 us (98%)
    pallas_call x1, Pallas kernels, local(): pl.pallas_call(kernel, out_shape=pltpu.VMEM((Q, COORDS + ROWS), F32), in_...  85.6 us

profile of v5, /device:TPU:1, one launch (start us, length us, event | category | flops | bytes accessed | tf_op | source)
XLA Modules:
  0.0 87.6 jit_solution(8345468614934549696)
XLA Ops:
  0.6 85.6 %logra.1 = f32[32,1536]{1,0:T(8,128)S(1)} custom-call(bf16[1024,4096]{1,0:T(8,128)(2,1)} %q_hbm.1, bf16[1024,128]{1,0:T(8,128)(2,1)} %cot_hbm.1, s32[8,128]{1,0:T(8,128)} %bitcast.10, bf16[448,4096]{1,0:T(8,128)(2,1)} %bitcast.8, bf16[448,4096]{1,0:T(8,128)(2,1)} %bitcast.9, bf16[448,128]{1,0:T(8,128)(2,1)} %pin_hbm.1, bf16[128,128]{1,0:T(8,128)(2,1)} %pout_hbm.1, ...), custom_call_target="tpu_custom_call" | custom-call | tf_op jit(solution)/shard_map/logra/pallas_call | solution.py:527
  86.3 0.6 slice_bitcast_fusion
  86.9 0.7 multiply_bitcast_fusion

commit v6 on v5

--- a/solution.py
+++ b/solution.py
@@ -54,10 +54,19 @@
 def eliminated(matrix, target):
     n = matrix.shape[0]
     both = jnp.concatenate([matrix, target], axis=1)
-    lines = lax.broadcasted_iota(jnp.int32, both.shape, 0)
-    for k in range(n):
-        row = both[k : k + 1, :] / both[k : k + 1, k : k + 1]
-        both = jnp.where(lines == k, row, both - both[:, k : k + 1] * row)
+    shape = both.shape
+    lines = lax.broadcasted_iota(jnp.int32, shape, 0)
+    for k in range(0, n, 2):
+        one = jnp.broadcast_to(both[:, k : k + 1], shape)
+        two = jnp.broadcast_to(both[:, k + 1 : k + 2], shape)
+        pivot = 1.0 / one[k : k + 1]
+        row = both[k : k + 1] * pivot
+        ratio = two[k : k + 1] * pivot
+        below = one[k + 1 : k + 2]
+        last = (both[k + 1 : k + 2] - below * row) / (two[k + 1 : k + 2] - below * ratio)
+        row = row - ratio * last
+        rest = both - one * row - two * last
+        both = jnp.where(lines == k, row, jnp.where(lines == k + 1, last, rest))
     return both[:, n:]
 
 
@@ -469,35 +478,31 @@
 
         lax.fori_loop(0, Q, line, 0)
 
-    blocks1 = rows_of(1)
-    own_packed(s1, blocks1)
-    arrived("c1")
-    dbuf[g] = summed([cbuf[s] for s in range(EX)])
-    push("c2", lambda p: dbuf.at[g], dbuf.at[g], g, GROUP, in_group, dbuf.at[pl.ds(0, GROUP - 1)])
-    spread(1, s1, (("sb", 1, 4),))
     arrived("ma")
     pending["mx"] = far.at[pl.ds(0, 3)]
     for dx in (2, 1, 3):
         send("mx", far.at[x], far.at[x], {"co": (x + dx) % 4})
+    blocks1 = rows_of(1)
+    own_packed(s1, blocks1)
+    spread(1, s1, (("sb", 1, 4),))
+    arrived("c1")
+    dbuf[g] = summed([cbuf[s] for s in range(EX)])
+    push("c2", lambda p: dbuf.at[g], dbuf.at[g], g, GROUP, in_group, dbuf.at[pl.ds(0, GROUP - 1)])
     gram = (
         norm1
         + fdot(cross, mixing)
         + fdot(mixing, cross, ((0,), (1,)))
         + fdot(mixing, fdot(norm0, mixing), TN)
     )
+    spare = fdot(mixing, fdot(row_gram, mixing), TN)
     arrived("fa0")
     arrived("fb0")
     pick(s0, 0)
+    forward(1, s1, "b")
     arrived("c2")
     total = summed([dbuf[s] for s in range(GROUP)])
     square, mixed = unfolded(total[:8]), unfolded(total[8:])
-    rows_gram = (
-        square
-        + fdot(mixed, mixing)
-        + fdot(mixing, mixed, ((0,), (1,)))
-        + fdot(mixing, fdot(row_gram, mixing), TN)
-    )
-    forward(1, s1, "b")
+    rows_gram = square + fdot(mixed, mixing) + fdot(mixing, mixed, ((0,), (1,))) + spare
     step1 = eliminated(rows_gram * (scale * scale) + DAMPING * gram, norm1)
     arrived("mx")
     for slot in range(4, 8):
@@ -506,13 +511,15 @@
     forward(1, s1, "a")
     first = step0 + fdot(mixing, step1)
     out_ref[:, :COORDS] = fdot(first, base, TN) + fdot(step1, residual, TN)
+    mask = mask_v[...]
+    across = ((0,), (1,))
+    scores = three_pass(jnp.concatenate([first] * 4, axis=0), picked[0] * mask, across)
     arrived("fa1")
     arrived("fb1")
     pick(s1, 1)
-    mask = mask_v[...]
-    chosen = jnp.concatenate([picked[0] * mask, picked[1] * mask], axis=1)
-    coeffs = jnp.concatenate([first] * 4 + [step1] * 4, axis=0)
-    out_ref[:, COORDS:] = three_pass(coeffs, chosen, ((0,), (1,)))
+    out_ref[:, COORDS:] = scores + three_pass(
+        jnp.concatenate([step1] * 4, axis=0), picked[1] * mask, across
+    )
 
     for phase in list(pending):
         sent(phase)

time: 87.7 us -> 87.9 us (level)
  no operation moved by 1% of the time
where the time goes in v6:
time: 87.9 us; the launch traced here: 87.8 us
  Pallas kernels  85.9 us (98%)
    pallas_call x1, Pallas kernels, local(): pl.pallas_call(kernel, out_shape=pltpu.VMEM((Q, COORDS + ROWS), F32), in_...  85.9 us

profile of v6, /device:TPU:1, one launch (start us, length us, event | category | flops | bytes accessed | tf_op | source)
XLA Modules:
  0.0 87.8 jit_solution(11522901469954394341)
XLA Ops:
  0.6 85.9 %logra.1 = f32[32,1536]{1,0:T(8,128)S(1)} custom-call(bf16[1024,4096]{1,0:T(8,128)(2,1)} %q_hbm.1, bf16[1024,128]{1,0:T(8,128)(2,1)} %cot_hbm.1, s32[8,128]{1,0:T(8,128)} %bitcast.10, bf16[448,4096]{1,0:T(8,128)(2,1)} %bitcast.8, bf16[448,4096]{1,0:T(8,128)(2,1)} %bitcast.9, bf16[448,128]{1,0:T(8,128)(2,1)} %pin_hbm.1, bf16[128,128]{1,0:T(8,128)(2,1)} %pout_hbm.1, ...), custom_call_target="tpu_custom_call" | custom-call | tf_op jit(solution)/shard_map/logra/pallas_call | solution.py:534
  86.5 0.6 slice_bitcast_fusion
  87.2 0.7 multiply_bitcast_fusion

commit v7 on v6

--- a/solution.py
+++ b/solution.py
@@ -32,8 +32,8 @@
 PHASES = (
     ["ids", "r1", "r2", "r3"]
     + [f"l1{c}" for c in range(CHUNKS)]
-    + ["l2", "gz", "b", "z1", "zg", "z3", "c1", "c2", "ma", "mx"]
-    + [f"{name}{k}" for name in ("y1", "y2", "y3", "g1", "g2", "sa", "sb", "fa", "fb") for k in (0, 1)]
+    + ["l2", "gz", "b", "z1", "zg", "z3", "c1", "c2"]
+    + [f"{name}{k}" for name in ("y1", "y2", "y3", "g1", "g2", "ma", "mx", "sb", "fa", "fb") for k in (0, 1)]
 )
 FAR_FIRST = {4: (2, 1), 5: (1, 1), 6: (3, 1), 7: (2, 0), 1: (1, 0), 2: (3, 0), 3: (0, 1)}
 PHASE = {name: at for at, name in enumerate(PHASES)}
@@ -395,13 +395,32 @@
     def half(d, count=1):
         return pl.ds(pl.multiple_of(core * ROWS + d * R, R), count * R)
 
-    def spread(k, buf, parts):
-        for name, lo, hi in parts:
-            pending[f"{name}{k}"] = buf.at[half(lo, hi - lo), :]
-            for slot in range(lo, hi):
-                dy, dz = FAR_FIRST[slot]
-                p = ((y - dy) % 4) * 2 + (z_lo + dz) % 2
-                send(f"{name}{k}", buf.at[half(0), :], buf.at[half(slot), :], in_ex(p))
+    def ex_peer(slot):
+        dy, dz = FAR_FIRST[slot]
+        return in_ex(((y - dy) % 4) * 2 + (z_lo + dz) % 2)
+
+    def near_rows(k, buf):
+        pending[f"sb{k}"] = buf.at[half(1, 3), :]
+        for slot in range(1, 4):
+            send(f"sb{k}", buf.at[half(0), :], buf.at[half(slot), :], ex_peer(slot))
+
+    def far_blocks(k):
+        pending[f"ma{k}"] = far.at[k, 0]
+        for slot in range(4, 8):
+            send(f"ma{k}", yfull.at[k, g], far.at[k, x, slot - 4], ex_peer(slot))
+
+    def far_rows(k):
+        arrived(f"ma{k}")
+        pending[f"mx{k}"] = far.at[k, pl.ds(0, 3)]
+        for dx in (2, 1, 3):
+            send(f"mx{k}", far.at[k, x], far.at[k, x], {"co": (x + dx) % 4})
+
+    def far_packed(k, buf):
+        arrived(f"mx{k}")
+        for slot in range(4, 8):
+            tall = jnp.concatenate([far[k, s, slot - 4] for s in range(4)], axis=0)
+            buf[half(slot), :] = tall.T
+        forward(k, buf, "a")
 
     def forward(k, buf, name):
         lo, hi = (4, 8) if name == "a" else (1, 4)
@@ -416,6 +435,7 @@
     second_stage(0)
     second_grams(0, 1)
     third_stage(0)
+    far_blocks(0)
     (norm0,) = grams_of(0, 1)
     eye = (
         lax.broadcasted_iota(jnp.int32, (Q, Q), 0) == lax.broadcasted_iota(jnp.int32, (Q, Q), 1)
@@ -429,6 +449,7 @@
         zsend[p] = back[16 * (p // 4) : 16 * (p // 4) + 16, (p % 4) * R : (p % 4 + 1) * R]
     push("z1", lambda p: zsend.at[p], z1.at[e], e, EX, in_ex, z1.at[pl.ds(0, EX - 1)])
     z1[e] = zsend[e]
+    far_rows(0)
     zg[e] = folded(repeated_gram(rows0, rows0))
     push("zg", lambda p: zg.at[e], zg.at[e], e, EX, in_ex, zg.at[pl.ds(0, EX - 1)])
     own_packed(s0, blocks0)
@@ -438,8 +459,9 @@
     arrived("zg")
     row_gram = unfolded(summed([zg[s] for s in range(EX)]))
     step0 = eliminated(row_gram * (scale * scale) + DAMPING * norm0, norm0)
+    far_packed(0, s0)
     arrived("z3")
-    spread(0, s0, (("sa", 4, 8), ("sb", 1, 4)))
+    near_rows(0, s0)
     back = jnp.concatenate(
         [jnp.concatenate([zfull[4 * h + j] for j in range(4)], axis=1) for h in range(2)], axis=0
     )
@@ -452,15 +474,8 @@
     )
     second_stage(1)
     second_grams(1, 2)
-    forward(0, s0, "a")
-    forward(0, s0, "b")
-    to_scalar.wait()
     third_stage(1)
-    pending["ma"] = far.at[0]
-    for slot in range(4, 8):
-        dy, dz = FAR_FIRST[slot]
-        p = ((y - dy) % 4) * 2 + (z_lo + dz) % 2
-        send("ma", yfull.at[1, g], far.at[x, slot - 4], in_ex(p))
+    far_blocks(1)
     block0, block1 = yfull[0, g], yfull[1, g]
     cbuf[e] = jnp.concatenate(
         [folded(repeated_gram(block1, block1)), folded(repeated_gram(block1, block0))], axis=0
@@ -478,13 +493,12 @@
 
         lax.fori_loop(0, Q, line, 0)
 
-    arrived("ma")
-    pending["mx"] = far.at[pl.ds(0, 3)]
-    for dx in (2, 1, 3):
-        send("mx", far.at[x], far.at[x], {"co": (x + dx) % 4})
+    forward(0, s0, "b")
+    to_scalar.wait()
+    far_rows(1)
     blocks1 = rows_of(1)
     own_packed(s1, blocks1)
-    spread(1, s1, (("sb", 1, 4),))
+    near_rows(1, s1)
     arrived("c1")
     dbuf[g] = summed([cbuf[s] for s in range(EX)])
     push("c2", lambda p: dbuf.at[g], dbuf.at[g], g, GROUP, in_group, dbuf.at[pl.ds(0, GROUP - 1)])
@@ -504,11 +518,7 @@
     square, mixed = unfolded(total[:8]), unfolded(total[8:])
     rows_gram = square + fdot(mixed, mixing) + fdot(mixing, mixed, ((0,), (1,))) + spare
     step1 = eliminated(rows_gram * (scale * scale) + DAMPING * gram, norm1)
-    arrived("mx")
-    for slot in range(4, 8):
-        tall = jnp.concatenate([far[s, slot - 4] for s in range(4)], axis=0)
-        s1[half(slot), :] = tall.T
-    forward(1, s1, "a")
+    far_packed(1, s1)
     first = step0 + fdot(mixing, step1)
     out_ref[:, :COORDS] = fdot(first, base, TN) + fdot(step1, residual, TN)
     mask = mask_v[...]
@@ -570,7 +580,7 @@
             pltpu.VMEM((EX, 16, R), F32),
             pltpu.VMEM((EX, 16, R), F32),
             pltpu.VMEM((GROUP, 16, R), F32),
-            pltpu.VMEM((4, 4, Q, R), F32),
+            pltpu.VMEM((2, 4, 4, Q, R), F32),
             pltpu.VMEM((2 * ROWS, R), F32),
             pltpu.VMEM((2 * ROWS, R), F32),
             pltpu.VMEM((2, ROWS, R), F32),

time: 87.9 us -> 87.1 us (level)
  no operation moved by 1% of the time
where the time goes in v7:
time: 87.1 us
  Pallas kernels  85.1 us (98%)
    pallas_call x1, Pallas kernels, local(): pl.pallas_call(kernel, out_shape=pltpu.VMEM((Q, COORDS + ROWS), F32), in_...  85.1 us

profile of v7, /device:TPU:1, one launch (start us, length us, event | category | flops | bytes accessed | tf_op | source)
XLA Modules:
  0.0 87.1 jit_solution(7011759665736586857)
XLA Ops:
  0.6 85.1 %logra.1 = f32[32,1536]{1,0:T(8,128)S(1)} custom-call(bf16[1024,4096]{1,0:T(8,128)(2,1)} %q_hbm.1, bf16[1024,128]{1,0:T(8,128)(2,1)} %cot_hbm.1, s32[8,128]{1,0:T(8,128)} %bitcast.10, bf16[448,4096]{1,0:T(8,128)(2,1)} %bitcast.8, bf16[448,4096]{1,0:T(8,128)(2,1)} %bitcast.9, bf16[448,128]{1,0:T(8,128)(2,1)} %pin_hbm.1, bf16[128,128]{1,0:T(8,128)(2,1)} %pout_hbm.1, ...), custom_call_target="tpu_custom_call" | custom-call | tf_op jit(solution)/shard_map/logra/pallas_call | solution.py:544
  85.8 0.6 slice_bitcast_fusion
  86.4 0.7 multiply_bitcast_fusion

commit v8 on v7

--- a/solution.py
+++ b/solution.py
@@ -9,6 +9,7 @@
 from jax.sharding import PartitionSpec as P
 
 D = 4096
+HALF = D // 2
 FFL = 448
 TOK = 1024
 CHUNK = 256
@@ -33,7 +34,7 @@
     ["ids", "r1", "r2", "r3"]
     + [f"l1{c}" for c in range(CHUNKS)]
     + ["l2", "gz", "b", "z1", "zg", "z3", "c1", "c2"]
-    + [f"{name}{k}" for name in ("y1", "y2", "y3", "g1", "g2", "ma", "mx", "sb", "fa", "fb") for k in (0, 1)]
+    + [f"{name}{k}" for name in ("y1", "y2", "y3", "g1", "g2", "ma", "mx", "my", "sb", "fa", "fb", "fc") for k in (0, 1)]
 )
 FAR_FIRST = {4: (2, 1), 5: (1, 1), 6: (3, 1), 7: (2, 0), 1: (1, 0), 2: (3, 0), 3: (0, 1)}
 PHASE = {name: at for at, name in enumerate(PHASES)}
@@ -172,9 +173,14 @@
         pltpu.make_async_copy(qot_hbm, qot_v, small_sem.at[3]),
         pltpu.make_async_copy(pin_hbm, pin_v, small_sem.at[4]),
         pltpu.make_async_copy(db_hbm, db_v, small_sem.at[5]),
-        pltpu.make_async_copy(gw_hbm, gw_v, w_sem.at[0]),
-        pltpu.make_async_copy(uw_hbm, uw_v, w_sem.at[1]),
     ]
+
+    for depth in range(2):
+        cols = pl.ds(depth * HALF, HALF)
+        for side, (src, dst) in enumerate(((gw_hbm, gw_v), (uw_hbm, uw_v))):
+            copies.append(
+                pltpu.make_async_copy(src.at[:, cols], dst.at[:, cols], w_sem.at[2 * depth + side])
+            )
 
     def q_copy(c):
         rows = pl.ds(c * CHUNK, CHUNK)
@@ -188,8 +194,8 @@
     for at in (0, 1, 2, 4):
         copies[at].start()
     q_copy(0).start()
-    copies[6].start()
-    copies[7].start()
+    for at in (6, 7, 8, 9):
+        copies[at].start()
     for c in range(1, CHUNKS):
         q_copy(c).start()
     copies[3].start()
@@ -214,14 +220,22 @@
     moved = old == 32 * ((new >> 2) & 3) + 4 * (new >> 4) + (new & 3)
     proj = bdot(pin_v[...], jnp.where(moved, 1.0, 0.0).astype(BF16))
     pin_v[...] = proj.astype(BF16)
-    copies[6].wait()
-    copies[7].wait()
 
     def matmul(c):
         q_copy(c).wait()
         a = q_v[c * CHUNK : (c + 1) * CHUNK, :]
-        gate = bdot(gw_v[...], a, NT)
-        up = bdot(uw_v[...], a, NT)
+        if c == 0:
+            copies[6].wait()
+            copies[7].wait()
+            gate = bdot(gw_v[:, :HALF], a[:, :HALF], NT)
+            up = bdot(uw_v[:, :HALF], a[:, :HALF], NT)
+            copies[8].wait()
+            copies[9].wait()
+            gate = gate + bdot(gw_v[:, HALF:], a[:, HALF:], NT)
+            up = up + bdot(uw_v[:, HALF:], a[:, HALF:], NT)
+        else:
+            gate = bdot(gw_v[...], a, NT)
+            up = bdot(uw_v[...], a, NT)
         hidden = ((gate / (1.0 + jnp.exp(-gate))) * up).astype(BF16)
         lsend[c] = bdot(pin_v[...], hidden, TN).reshape(GROUP, 16, CHUNK)
         push(
@@ -246,11 +260,11 @@
     matmul(0)
     matmul(1)
     matmul(2)
+    matmul(3)
     arrived("r1")
     r2s[...] = summed([r1[s] for s in range(GROUP)])
     push("r2", lambda p: r2s.at[p], r2.at[zh], zh, ZH, in_z, r2.at[pl.ds(0, ZH - 1)])
     r2[zh] = r2s[zh]
-    matmul(3)
     left_second(0)
     left_second(1)
     left_second(2)
@@ -411,19 +425,21 @@
 
     def far_rows(k):
         arrived(f"ma{k}")
-        pending[f"mx{k}"] = far.at[k, pl.ds(0, 3)]
-        for dx in (2, 1, 3):
-            send(f"mx{k}", far.at[k, x], far.at[k, x], {"co": (x + dx) % 4})
+        for name, pair in (("mx", pl.ds(0, 2)), ("my", pl.ds(2, 2))):
+            pending[f"{name}{k}"] = far.at[k, pl.ds(0, 3), pair]
+            for dx in (2, 1, 3):
+                send(f"{name}{k}", far.at[k, x, pair], far.at[k, x, pair], {"co": (x + dx) % 4})
 
     def far_packed(k, buf):
-        arrived(f"mx{k}")
-        for slot in range(4, 8):
-            tall = jnp.concatenate([far[k, s, slot - 4] for s in range(4)], axis=0)
-            buf[half(slot), :] = tall.T
-        forward(k, buf, "a")
+        for name, lo, onward in (("mx", 4, "a"), ("my", 6, "c")):
+            arrived(f"{name}{k}")
+            for slot in range(lo, lo + 2):
+                tall = jnp.concatenate([far[k, s, slot - 4] for s in range(4)], axis=0)
+                buf[half(slot), :] = tall.T
+            forward(k, buf, onward)
 
     def forward(k, buf, name):
-        lo, hi = (4, 8) if name == "a" else (1, 4)
+        lo, hi = {"a": (4, 6), "c": (6, 8), "b": (1, 4)}[name]
         if f"s{name}{k}" in pending:
             arrived(f"s{name}{k}")
         part = buf.at[half(lo, hi - lo), :]
@@ -510,6 +526,7 @@
     )
     spare = fdot(mixing, fdot(row_gram, mixing), TN)
     arrived("fa0")
+    arrived("fc0")
     arrived("fb0")
     pick(s0, 0)
     forward(1, s1, "b")
@@ -525,6 +542,7 @@
     across = ((0,), (1,))
     scores = three_pass(jnp.concatenate([first] * 4, axis=0), picked[0] * mask, across)
     arrived("fa1")
+    arrived("fc1")
     arrived("fb1")
     pick(s1, 1)
     out_ref[:, COORDS:] = scores + three_pass(
@@ -589,7 +607,7 @@
             pltpu.SMEM((Q, R), jnp.int32),
             pltpu.SemaphoreType.DMA((7,)),
             pltpu.SemaphoreType.DMA((CHUNKS,)),
-            pltpu.SemaphoreType.DMA((2,)),
+            pltpu.SemaphoreType.DMA((4,)),
             pltpu.SemaphoreType.DMA((len(PHASES),)),
             pltpu.SemaphoreType.DMA((len(PHASES),)),
         ],

time: 87.1 us -> 89.1 us (1.023)
  Pallas kernels: 85.1 us -> 87 us
    pallas_call x1, Pallas kernels: 85.1 us -> 87 us  [local(): pl.pallas_call(kernel, out_shape=pltpu.VMEM((Q, COORDS + ROWS), F32), in_...]
where the time goes in v8:
time: 89.1 us; the launch traced here: 89 us
  Pallas kernels  87 us (98%)
    pallas_call x1, Pallas kernels, local(): pl.pallas_call(kernel, out_shape=pltpu.VMEM((Q, COORDS + ROWS), F32), in_...  87 us

profile of v8, /device:TPU:1, one launch (start us, length us, event | category | flops | bytes accessed | tf_op | source)
XLA Modules:
  0.0 89.0 jit_solution(18351369567029079804)
XLA Ops:
  0.6 87.0 %logra.1 = f32[32,1536]{1,0:T(8,128)S(1)} custom-call(bf16[1024,4096]{1,0:T(8,128)(2,1)} %q_hbm.1, bf16[1024,128]{1,0:T(8,128)(2,1)} %cot_hbm.1, s32[8,128]{1,0:T(8,128)} %bitcast.10, bf16[448,4096]{1,0:T(8,128)(2,1)} %bitcast.8, bf16[448,4096]{1,0:T(8,128)(2,1)} %bitcast.9, bf16[448,128]{1,0:T(8,128)(2,1)} %pin_hbm.1, bf16[128,128]{1,0:T(8,128)(2,1)} %pout_hbm.1, ...), custom_call_target="tpu_custom_call" | custom-call | tf_op jit(solution)/shard_map/logra/pallas_call | solution.py:562
  87.7 0.6 slice_bitcast_fusion
  88.3 0.7 multiply_bitcast_fusion

commit v9 on v8

--- a/solution.py
+++ b/solution.py
@@ -260,11 +260,11 @@
     matmul(0)
     matmul(1)
     matmul(2)
-    matmul(3)
     arrived("r1")
     r2s[...] = summed([r1[s] for s in range(GROUP)])
     push("r2", lambda p: r2s.at[p], r2.at[zh], zh, ZH, in_z, r2.at[pl.ds(0, ZH - 1)])
     r2[zh] = r2s[zh]
+    matmul(3)
     left_second(0)
     left_second(1)
     left_second(2)

time: 89.1 us -> 86.9 us (0.975)
  Pallas kernels: 87 us -> 84.8 us
    pallas_call x1, Pallas kernels: 87 us -> 84.8 us  [local(): pl.pallas_call(kernel, out_shape=pltpu.VMEM((Q, COORDS + ROWS), F32), in_...]
where the time goes in v9:
time: 86.9 us; the launch traced here: 86.8 us
  Pallas kernels  84.8 us (98%)
    pallas_call x1, Pallas kernels, local(): pl.pallas_call(kernel, out_shape=pltpu.VMEM((Q, COORDS + ROWS), F32), in_...  84.8 us

profile of v9, /device:TPU:1, one launch (start us, length us, event | category | flops | bytes accessed | tf_op | source)
XLA Modules:
  0.0 86.8 jit_solution(10814067625714691555)
XLA Ops:
  0.6 84.8 %logra.1 = f32[32,1536]{1,0:T(8,128)S(1)} custom-call(bf16[1024,4096]{1,0:T(8,128)(2,1)} %q_hbm.1, bf16[1024,128]{1,0:T(8,128)(2,1)} %cot_hbm.1, s32[8,128]{1,0:T(8,128)} %bitcast.10, bf16[448,4096]{1,0:T(8,128)(2,1)} %bitcast.8, bf16[448,4096]{1,0:T(8,128)(2,1)} %bitcast.9, bf16[448,128]{1,0:T(8,128)(2,1)} %pin_hbm.1, bf16[128,128]{1,0:T(8,128)(2,1)} %pout_hbm.1, ...), custom_call_target="tpu_custom_call" | custom-call | tf_op jit(solution)/shard_map/logra/pallas_call | solution.py:562
  85.5 0.6 slice_bitcast_fusion
  86.1 0.7 multiply_bitcast_fusion
